TPU v7x, 128 devices: a whole 4x4x4 slice. The times are simulated.
128 devices in a mesh: row: 4 (over z), col: 16 (over x, y), gz: 2 (over core).
Axes of the slice: x: 4, y: 4, z: 4, core: 2. Of those that a mesh axis runs over, the one named last changes fastest.
Arguments:
- rhs_half: float32 [2, 3, 64, 4096], P('gz', None, None, ('row', 'col')), may hold values from -6 to 6
- rhs_root: float32 [64, 4096], P(None, ('row', 'col')), may hold values from -6 to 6
- lower_coupling: bfloat16 [2, 5, 4096, 4096], P('gz', None, 'col', 'row'), may hold values from -0.046875 to 0.046875
- lower_pattern: int32 [2, 5, 32, 32], P('gz', None, 'col', 'row'), may hold values 0 or 1
- upper_coupling: bfloat16 [2, 5, 4096, 4096], P('gz', None, 'col', 'row'), may hold values from -0.046875 to 0.046875
- upper_pattern: int32 [2, 5, 32, 32], P('gz', None, 'col', 'row'), may hold values 0 or 1
- lower_inverse: bfloat16 [2, 3, 4096, 4096], P('gz', None, 'col', 'row'), may hold values from -0.09375 to 0.09375
- upper_inverse: bfloat16 [2, 3, 4096, 4096], P('gz', None, 'col', 'row'), may hold values from -0.09375 to 0.09375
- root_lower_inverse: bfloat16 [4096, 4096], P('col', 'row'), may hold values from -0.09375 to 0.09375
- root_upper_inverse: bfloat16 [4096, 4096], P('col', 'row'), may hold values from -0.09375 to 0.09375
Outputs:
- sol_half: float32 [2, 3, 64, 4096], P('gz', None, None, ('row', 'col'))
- sol_root: float32 [64, 4096], P(None, ('row', 'col'))
All inputs are finite; a program needn't handle non-finite values. No bound on the sum of `lower_pattern` or of `upper_pattern` on one device may be relied on, other than what follows from the above.
Results may differ from a plain program's by a relative error of at most 0.007.
Values may be sent and summed in bfloat16 or wider, within the bound.
A program may use at most 64 MiB of HBM per device.

v0:
```python
import jax
import jax.numpy as jnp
from jax import lax
from jax.sharding import PartitionSpec as P


def apply_mask(tiles, pattern):
    count, across, down = pattern.shape
    shaped = tiles.reshape(count, across, tiles.shape[1] // across, down, tiles.shape[2] // down)
    shaped = shaped * pattern[:, :, None, :, None].astype(jnp.bfloat16)
    return shaped.reshape(tiles.shape)


def multiply(vectors, tiles):
    return jnp.einsum("snj,sji->sni", vectors, tiles, preferred_element_type=jnp.float32)


def multiply_one(vectors, tiles):
    return jnp.einsum("nj,sji->sni", vectors[0], tiles, preferred_element_type=jnp.float32)


def settle(partial_value, offset_bias, column, narrow):
    share_width = offset_bias.shape[2]
    slot = (
        lax.dynamic_slice_in_dim(partial_value, column * share_width, share_width, 2) + offset_bias
    )
    partial_value = lax.dynamic_update_slice_in_dim(partial_value, slot, column * share_width, 2)
    summed = lax.psum(partial_value, "col")
    owned = lax.dynamic_slice_in_dim(summed, column * share_width, share_width, 2)
    gathered = lax.all_gather(summed.astype(jnp.bfloat16), "row", axis=2, tiled=True)
    return (owned, lax.dynamic_slice_in_dim(gathered, column * narrow, narrow, 2))


def per_device(
    rhs_half,
    rhs_root,
    lower_coupling,
    lower_pattern,
    upper_coupling,
    upper_pattern,
    lower_inverse,
    upper_inverse,
    root_lower_inverse,
    root_upper_inverse,
):
    column = lax.axis_index("col")
    lower = apply_mask(lower_coupling[0], lower_pattern[0])
    upper = apply_mask(upper_coupling[0], upper_pattern[0])
    narrow = lower.shape[1]
    share_width = rhs_half.shape[3]
    nrhs_count = rhs_half.shape[2]

    def zeros_for(count):
        return jnp.zeros((count, nrhs_count, share_width), jnp.float32)

    leaf_full = lax.all_gather(
        rhs_half[0, 1:3].astype(jnp.bfloat16), ("row", "col"), axis=2, tiled=True
    )
    leaf_input = lax.dynamic_slice_in_dim(leaf_full, column * narrow, narrow, 2)
    leaf_value, leaf_cols = settle(
        multiply(leaf_input, lower_inverse[0, 1:3]), zeros_for(2), column, narrow
    )
    top_terms = -multiply(leaf_cols, lower[0:2]).sum(axis=0, keepdims=True)
    top_rest, top_input = settle(top_terms, rhs_half[0, 0:1], column, narrow)
    top_value, top_cols = settle(
        multiply(top_input, lower_inverse[0, 0:1]), zeros_for(1), column, narrow
    )
    every_cols = jnp.concatenate([top_cols, leaf_cols], axis=0)
    root_terms = -multiply(every_cols, lower[2:5]).sum(axis=0, keepdims=True)
    root_terms = lax.psum(root_terms, "gz")
    root_rest, root_input = settle(root_terms, rhs_root[None], column, narrow)
    root_value, root_cols = settle(
        multiply(root_input, root_lower_inverse[None]), zeros_for(1), column, narrow
    )
    root_back, root_back_cols = settle(
        multiply(root_cols, root_upper_inverse[None]), zeros_for(1), column, narrow
    )
    first_terms = -multiply_one(root_back_cols, upper[2:3])
    first_rest, first_input = settle(first_terms, top_value, column, narrow)
    first_back, first_back_cols = settle(
        multiply(first_input, upper_inverse[0, 0:1]), zeros_for(1), column, narrow
    )
    second_terms = -(
        multiply_one(root_back_cols, upper[3:5]) + multiply_one(first_back_cols, upper[0:2])
    )
    second_rest, second_input = settle(second_terms, leaf_value, column, narrow)
    second_back, second_back_cols = settle(
        multiply(second_input, upper_inverse[0, 1:3]), zeros_for(2), column, narrow
    )
    sol_half = jnp.concatenate([first_back, second_back], axis=0)[None]
    return (sol_half, root_back[0])


def solution(mesh):
    in_specs = (
        P("gz", None, None, ("row", "col")),
        P(None, ("row", "col")),
        P("gz", None, "col", "row"),
        P("gz", None, "col", "row"),
        P("gz", None, "col", "row"),
        P("gz", None, "col", "row"),
        P("gz", None, "col", "row"),
        P("gz", None, "col", "row"),
        P("col", "row"),
        P("col", "row"),
    )
    out_specs = (P("gz", None, None, ("row", "col")), P(None, ("row", "col")))
    return jax.shard_map(
        per_device, mesh=mesh, in_specs=in_specs, out_specs=out_specs, check_vma=False
    )
```

profile of v0, /device:TPU:0, one launch (start us, length us, event | category | flops | bytes accessed | tf_op | source)
XLA Modules:
  0.0 1071.1 jit_solution(17997548227670011957)
XLA Ops:
  9.0 70.3 %all-gather.9.cloned.1.call-done = bf16[1,2,64,4096]{2,1,0,3:T(2,128)(2,1)} async-done(((bf16[1,2,64,64]{2,1,0,3:T(2,128)(2,1)}), bf16[1,2,64,4096]{2,1,0,3:T(2,128)(2,1)}) %all-gather.9.cloned.1.call-update) | async-done | bytes 1048592 | tf_op jit(solution)/shard_map/all_gather | solution.py:56
  80.4 1.5 fusion.6
  82.9 1.6 dynamic_update_slice.30
  84.5 83.1 %all-reduce.12.cloned.1.call-done = f32[2,64,1024]{2,1,0:T(8,128)} async-done(((f32[2,64,1024]{2,1,0:T(8,128)}), f32[2,64,1024]{2,1,0:T(8,128)}) %all-reduce.12.cloned.1.call-update) | async-done | bytes 524304 | tf_op jit(solution)/shard_map/psum | solution.py:28
  167.6 1.8 convert_element_type.56
  171.4 2.3 slice.51
  173.7 19.6 %all-gather.5.cloned.1.call-done = bf16[2,64,4096]{2,1,0:T(8,128)(2,1)} async-done(((bf16[2,64,1024]{2,1,0:T(8,128)(2,1)}), bf16[2,64,4096]{2,1,0:T(8,128)(2,1)}) %all-gather.5.cloned.1.call-update) | async-done | bytes 1048592 | tf_op jit(solution)/shard_map/all_gather | solution.py:30
  194.2 1.5 fusion.1
  197.0 77.2 %all-reduce.23 = bf16[1,64,1024]{2,1,0:T(8,128)(2,1)} all-reduce(f32[1,64,1024]{2,1,0:T(8,128)S(1)} %dynamic_update_slice.31), channel_id=1, replica_groups=mesh['row'=4,'col'=16,'gz'=2] {'col'}, use_global_device_ids=true, to_apply=%region_1.0 | all-reduce | flops 65536 | bytes 393216 | tf_op jit(solution)/shard_map/psum | solution.py:28
  274.2 13.0 %all_gather.32 = bf16[1,64,4096]{2,1,0:T(8,128)(2,1)S(1)} all-gather(bf16[1,64,1024]{2,1,0:T(8,128)(2,1)} %all-reduce.23), channel_id=1, replica_groups=mesh['row'=4,'col'=16,'gz'=2] {'row'}, dimensions={2}, use_global_device_ids=true | all-gather | bytes 655360 | tf_op jit(solution)/shard_map/all_gather | solution.py:30
  291.0 2.5 slice.55
  293.5 3.9 copy.17
  297.4 72.5 %all-reduce.14.cloned.1.call-done = f32[1,64,1024]{2,1,0:T(8,128)} async-done(((f32[1,64,1024]{2,1,0:T(8,128)}), f32[1,64,1024]{2,1,0:T(8,128)}) %all-reduce.14.cloned.1.call-update) | async-done | bytes 262160 | tf_op jit(solution)/shard_map/psum | solution.py:28
  370.9 13.8 %all_gather.33 = bf16[1,64,4096]{2,1,0:T(8,128)(2,1)S(1)} all-gather(bf16[1,64,1024]{2,1,0:T(8,128)(2,1)S(1)} %convert_element_type.60), channel_id=1, replica_groups=mesh['row'=4,'col'=16,'gz'=2] {'row'}, dimensions={2}, use_global_device_ids=true | all-gather | bytes 655360 | tf_op jit(solution)/shard_map/all_gather | solution.py:30
  386.0 2.0 broadcast_multiply_fusion.1
  388.0 20.1 %all-reduce.16.cloned.1.call-done = f32[1,64,1024]{2,1,0:T(8,128)} async-done(((f32[1,64,1024]{2,1,0:T(8,128)}), f32[1,64,1024]{2,1,0:T(8,128)}) %all-reduce.16.cloned.1.call-update) | async-done | bytes 262160 | tf_op jit(solution)/shard_map/psum | solution.py:70
  410.4 77.5 %all-reduce.24 = bf16[1,64,1024]{2,1,0:T(8,128)(2,1)S(1)} all-reduce(f32[1,64,1024]{2,1,0:T(8,128)} %dynamic_update_slice.33), channel_id=1, replica_groups=mesh['row'=4,'col'=16,'gz'=2] {'col'}, use_global_device_ids=true, to_apply=%region_4.0 | all-reduce | flops 65536 | bytes 393216 | tf_op jit(solution)/shard_map/psum | solution.py:28
  487.9 13.3 %all_gather.34 = bf16[1,64,4096]{2,1,0:T(8,128)(2,1)S(1)} all-gather(bf16[1,64,1024]{2,1,0:T(8,128)(2,1)S(1)} %all-reduce.24), channel_id=1, replica_groups=mesh['row'=4,'col'=16,'gz'=2] {'row'}, dimensions={2}, use_global_device_ids=true | all-gather | bytes 655360 | tf_op jit(solution)/shard_map/all_gather | solution.py:30
  501.8 71.9 %all-reduce.25 = bf16[1,64,1024]{2,1,0:T(8,128)(2,1)S(1)} all-reduce(f32[1,64,1024]{2,1,0:T(8,128)S(1)} %dynamic_update_slice.34), channel_id=1, replica_groups=mesh['row'=4,'col'=16,'gz'=2] {'col'}, use_global_device_ids=true, to_apply=%region_5.0 | all-reduce | flops 65536 | bytes 393216 | tf_op jit(solution)/shard_map/psum | solution.py:28
  573.8 12.8 %all_gather.35 = bf16[1,64,4096]{2,1,0:T(8,128)(2,1)S(1)} all-gather(bf16[1,64,1024]{2,1,0:T(8,128)(2,1)S(1)} %all-reduce.25), channel_id=1, replica_groups=mesh['row'=4,'col'=16,'gz'=2] {'row'}, dimensions={2}, use_global_device_ids=true | all-gather | bytes 655360 | tf_op jit(solution)/shard_map/all_gather | solution.py:30
  592.1 1.6 slice.58
  593.7 77.1 %all-reduce.18.cloned.1.call-done = f32[1,64,1024]{2,1,0:T(8,128)} async-done(((f32[1,64,1024]{2,1,0:T(8,128)}), f32[1,64,1024]{2,1,0:T(8,128)}) %all-reduce.18.cloned.1.call-update) | async-done | bytes 262160 | tf_op jit(solution)/shard_map/psum | solution.py:28
  671.8 13.8 %all_gather.36 = bf16[1,64,4096]{2,1,0:T(8,128)(2,1)S(1)} all-gather(bf16[1,64,1024]{2,1,0:T(8,128)(2,1)S(1)} %convert_element_type.63), channel_id=1, replica_groups=mesh['row'=4,'col'=16,'gz'=2] {'row'}, dimensions={2}, use_global_device_ids=true | all-gather | bytes 655360 | tf_op jit(solution)/shard_map/all_gather | solution.py:30
  687.2 74.7 %all-reduce.26 = bf16[1,64,1024]{2,1,0:T(8,128)(2,1)S(1)} all-reduce(f32[1,64,1024]{2,1,0:T(8,128)S(1)} %dynamic_update_slice.36), channel_id=1, replica_groups=mesh['row'=4,'col'=16,'gz'=2] {'col'}, use_global_device_ids=true, to_apply=%region_7.0 | all-reduce | flops 65536 | bytes 393216 | tf_op jit(solution)/shard_map/psum | solution.py:28
  761.9 12.8 %all_gather.37 = bf16[1,64,4096]{2,1,0:T(8,128)(2,1)S(1)} all-gather(bf16[1,64,1024]{2,1,0:T(8,128)(2,1)S(1)} %all-reduce.26), channel_id=1, replica_groups=mesh['row'=4,'col'=16,'gz'=2] {'row'}, dimensions={2}, use_global_device_ids=true | all-gather | bytes 655360 | tf_op jit(solution)/shard_map/all_gather | solution.py:30
  777.2 1.9 fusion.24
  779.1 78.6 %all-reduce.20.cloned.1.call-done = f32[1,64,1024]{2,1,0:T(8,128)} async-done(((f32[1,64,1024]{2,1,0:T(8,128)}), f32[1,64,1024]{2,1,0:T(8,128)}) %all-reduce.20.cloned.1.call-update) | async-done | bytes 262160 | tf_op jit(solution)/shard_map/psum | solution.py:28
  858.7 13.8 %all_gather.38 = bf16[1,64,4096]{2,1,0:T(8,128)(2,1)S(1)} all-gather(bf16[1,64,1024]{2,1,0:T(8,128)(2,1)S(1)} %convert_element_type.65), channel_id=1, replica_groups=mesh['row'=4,'col'=16,'gz'=2] {'row'}, dimensions={2}, use_global_device_ids=true | all-gather | bytes 655360 | tf_op jit(solution)/shard_map/all_gather | solution.py:30
  875.3 78.4 %all-reduce.27 = bf16[2,64,1024]{2,1,0:T(8,128)(2,1)} all-reduce(f32[2,64,1024]{2,1,0:T(8,128)S(1)} %dynamic_update_slice.38), channel_id=1, replica_groups=mesh['row'=4,'col'=16,'gz'=2] {'col'}, use_global_device_ids=true, to_apply=%region_9.0 | all-reduce | flops 131072 | bytes 786432 | tf_op jit(solution)/shard_map/psum | solution.py:28
  953.7 20.4 %all-gather.7.cloned.1.call-done = bf16[2,64,4096]{2,1,0:T(8,128)(2,1)} async-done(((bf16[2,64,1024]{2,1,0:T(8,128)(2,1)}), bf16[2,64,4096]{2,1,0:T(8,128)(2,1)}) %all-gather.7.cloned.1.call-update) | async-done | bytes 1048592 | tf_op jit(solution)/shard_map/all_gather | solution.py:30
  974.1 1.6 fusion.4
  979.4 83.6 %all-reduce.22.cloned.1.call-done = f32[2,64,1024]{2,1,0:T(8,128)} async-done(((f32[2,64,1024]{2,1,0:T(8,128)}), f32[2,64,1024]{2,1,0:T(8,128)}) %all-reduce.22.cloned.1.call-update) | async-done | bytes 524304 | tf_op jit(solution)/shard_map/psum | solution.py:28
  (91 shorter events, 36.3 us)
Async XLA Ops:
  7.2 494.0 %copy-start = (bf16[256,1024]{1,0:T(8,128)(2,1)S(1)}, bf16[256,1024]{1,0:T(8,128)(2,1)}, u32[]{:S(2)}) copy-start(bf16[256,1024]{1,0:T(8,128)(2,1)} %param.18) | copy-start | bytes 1572868
  7.2 162.2 %copy-start.2 = (bf16[1,5,256,1024]{3,2,1,0:T(8,128)(2,1)S(1)}, bf16[1,5,256,1024]{3,2,1,0:T(8,128)(2,1)}, u32[]{:S(2)}) copy-start(bf16[1,5,256,1024]{3,2,1,0:T(8,128)(2,1)} %param.12) | copy-start | bytes 7864324
  7.2 72.2 %all-gather.9.cloned.1.call-start = ((), (), s32[]{:S(2)}) async-start(), calls=%async_computation.8 | async-start | bytes 2129920 | tf_op jit(solution)/shard_map/all_gather | solution.py:56
  9.0 158.6 %all-reduce.12.cloned.1.call-start = ((), (), s32[]{:S(2)}) async-start(), calls=%async_computation | async-start | bytes 1048576 | tf_op jit(solution)/shard_map/psum | solution.py:28
  82.0 0.8 copy-start.3
  84.4 108.9 %all-gather.5.cloned.1.call-start = ((), (), s32[]{:S(2)}) async-start(), calls=%async_computation.1 | async-start | bytes 1310720 | tf_op jit(solution)/shard_map/all_gather | solution.py:30
  169.4 200.6 %all-reduce.14.cloned.1.call-start = ((), (), s32[]{:S(2)}) async-start(), calls=%async_computation.2 | async-start | bytes 524288 | tf_op jit(solution)/shard_map/psum | solution.py:28
  169.4 0.7 copy-start.10
  288.9 0.7 copy-start.5
  289.6 118.4 %all-reduce.16.cloned.1.call-start = ((), (), s32[]{:S(2)}) async-start(), calls=%async_computation.3 | async-start | bytes 524288 | tf_op jit(solution)/shard_map/psum | solution.py:70
  293.5 3.9 copy-start.11
  385.9 285.0 %all-reduce.18.cloned.1.call-start = ((), (), s32[]{:S(2)}) async-start(), calls=%async_computation.4 | async-start | bytes 524288 | tf_op jit(solution)/shard_map/psum | solution.py:28
  386.0 22.1 %copy-start.9 = (f32[64,64]{1,0:T(8,128)S(1)}, f32[64,64]{1,0:T(8,128)}, u32[]{:S(2)}) copy-start(f32[64,64]{1,0:T(8,128)} %param.11) | copy-start | bytes 49156
  388.0 201.2 %copy-start.1 = (bf16[5,2,128,8,128]{4,3,2,1,0:T(8,128)(2,1)}, bf16[5,2,128,8,128]{4,3,2,1,0:T(8,128)(2,1)S(1)}, u32[]{:S(2)}) copy-start(bf16[5,2,128,8,128]{4,3,2,1,0:T(8,128)(2,1)S(1)} %broadcast_multiply_fusion.1) | copy-start | bytes 7864324
  588.3 0.7 copy-start.6
  589.1 268.7 %all-reduce.20.cloned.1.call-start = ((), (), s32[]{:S(2)}) async-start(), calls=%async_computation.5 | async-start | bytes 524288 | tf_op jit(solution)/shard_map/psum | solution.py:28
  592.1 93.5 %slice-start = ((bf16[5,2,128,8,128]{4,3,2,1,0:T(8,128)(2,1)}), bf16[1,2,128,8,128]{4,3,2,1,0:T(8,128)(2,1)S(1)}, s32[]{:S(2)}) async-start(bf16[5,2,128,8,128]{4,3,2,1,0:T(8,128)(2,1)} %copy-done.1), calls=%async_computation.9 | async-start | bytes 1048576 | tf_op jit(solution)/shard_map/slice | solution.py:78
  685.7 1.1 copy-start.8
  776.5 0.7 copy-start.7
  777.2 197.0 %all-gather.7.cloned.1.call-start = ((), (), s32[]{:S(2)}) async-start(), calls=%async_computation.6 | async-start | bytes 1310720 | tf_op jit(solution)/shard_map/all_gather | solution.py:30
  953.7 109.3 %all-reduce.22.cloned.1.call-start = ((), (), s32[]{:S(2)}) async-start(), calls=%async_computation.7 | async-start | bytes 1048576 | tf_op jit(solution)/shard_map/psum | solution.py:28
  976.3 0.8 copy-start.4
Sparse Core Ops, SparseCore 0:
  11.4 67.8 all-gather.8
  84.6 82.9 all-reduce.11
  169.5 23.8 all-gather.4
  289.8 80.1 all-reduce.13
  386.0 22.0 all-reduce.15
  589.2 81.6 all-reduce.17
  777.3 80.3 all-reduce.19
  953.8 20.2 all-gather.6
  977.3 85.5 all-reduce.21
where the time goes:
time: 1070 us
  waiting for transfers between devices  526 us (49%)
  blocking collectives  473 us (44%)
  local copies, waits for them, and re-layouts  33.8 us (3%)
  between operations  14.2 us (1%)
  matrix products  13.1 us (1%)
  other arithmetic  11 us (1%)
    psum x5, waiting for transfers between devices, settle(): summed = lax.psum(partial_value, 'col')  395 us
    psum x5, blocking collectives, settle(): summed = lax.psum(partial_value, 'col')  380 us
    all_gather x7, blocking collectives, settle(): lax.all_gather(summed.astype(jnp.bfloat16), 'row', axis=2, tiled=True)  93.3 us
    all_gather x1, waiting for transfers between devices, per_device(): lax.all_gather(rhs_half[0, 1:3].astype(jnp.bfloat16), ('row', 'col'), axi...  70.3 us
    all_gather x2, waiting for transfers between devices, settle(): lax.all_gather(summed.astype(jnp.bfloat16), 'row', axis=2, tiled=True)  40 us
  transfers between devices with their start and end apart: 9, of which 9 were waited for; matrix products, arithmetic and copies ran while one was open for 2% of the time, Pallas kernels for 0%

commit v1 on v0

v1 whole, which is shorter than its diff:
```python
import jax
import jax.numpy as jnp
from jax import lax
from jax.experimental import pallas as pl
from jax.experimental.pallas import tpu as pltpu
from jax.sharding import PartitionSpec as P

MESH = pl.DeviceIdType.MESH
F32 = jnp.float32
BF16 = jnp.bfloat16

NEAR = sorted(
    ((dx, dy) for dx in range(4) for dy in range(4) if dx or dy),
    key=lambda d: -(min(d[0], 4 - d[0]) + min(d[1], 4 - d[1])),
)


def dot(vector, tiles):
    return jnp.dot(vector, tiles, preferred_element_type=F32)


def add_up(ref, count):
    total = ref[0].astype(F32)
    for i in range(1, count):
        total = total + ref[i].astype(F32)
    return total


def kernel(
    rhs_half,
    rhs_root,
    lower_pattern,
    upper_pattern,
    lower_hbm,
    upper_hbm,
    lower_inverse_hbm,
    upper_inverse_hbm,
    root_lower_hbm,
    root_upper_hbm,
    sol_half,
    sol_root,
    lower,
    upper,
    lower_inverse,
    upper_inverse,
    root_lower,
    root_upper,
    leaf_pack,
    leaf_recv,
    bias_pack,
    bias_recv,
    send1,
    send2,
    send3,
    send4,
    send5,
    send6,
    send7,
    send8,
    send9,
    send10,
    recv1,
    recv2,
    recv3,
    recv4,
    recv5,
    recv6,
    recv7,
    recv8,
    recv9,
    recv10,
    part1,
    part2,
    part3,
    part4,
    part5,
    part6,
    part7,
    part8,
    part9,
    vec1,
    vec2,
    vec3,
    vec4,
    vec5,
    vec6,
    vec7,
    vec8,
    vec9,
    leaf_value,
    top_value,
    root_early,
    second_early,
    root_out,
    root_out_recv,
    first_out,
    first_out_recv,
    weight_sem,
    scatter_send,
    scatter_recv,
    spread_send,
    spread_recv,
    spread_self,
    misc_send,
    misc_recv,
    misc_self,
):
    z = lax.axis_index("row")
    col = lax.axis_index("col")
    core = lax.axis_index("gz")
    x = col // 4
    y = col % 4
    other = 1 - core

    def start_local(src, dst, sem):
        pltpu.make_async_copy(src, dst, sem).start()

    def wait_for(ref, sem):
        pltpu.make_async_copy(ref, ref, sem).wait()

    def send(src, dst, send_sem, recv_sem, device):
        pltpu.make_async_remote_copy(
            src_ref=src,
            dst_ref=dst,
            send_sem=send_sem,
            recv_sem=recv_sem,
            device_id=device,
            device_id_type=MESH,
        ).start()

    def send_or_keep(here, src, dst, send_sem, recv_sem, device):
        @pl.when(jnp.logical_not(here))
        def _():
            send(src, dst, send_sem, recv_sem, device)

        @pl.when(here)
        def _():
            start_local(src, dst, recv_sem)

    def wait_sent_unless(here, ref, sem):
        @pl.when(jnp.logical_not(here))
        def _():
            wait_for(ref, sem)

    start_local(lower_inverse_hbm, lower_inverse, weight_sem.at[0])
    start_local(lower_hbm, lower, weight_sem.at[1])
    for j in range(4):
        columns = pl.ds(pl.multiple_of(256 * j + 128 * core, 128), 128)
        start_local(
            root_lower_hbm.at[:, columns], root_lower.at[:, pl.ds(128 * j, 128)], weight_sem.at[2]
        )
    for j in range(4):
        columns = pl.ds(pl.multiple_of(256 * j + 128 * core, 128), 128)
        start_local(
            root_upper_hbm.at[:, columns], root_upper.at[:, pl.ds(128 * j, 128)], weight_sem.at[3]
        )
    start_local(upper_hbm, upper, weight_sem.at[4])
    start_local(upper_inverse_hbm, upper_inverse, weight_sem.at[5])

    barrier = pltpu.get_barrier_semaphore()

    def greet(px, py, pz, pcore):
        pl.semaphore_signal(
            barrier, inc=1, device_id=(pz, 4 * px + py, pcore), device_id_type=MESH
        )

    @pl.when(x != z)
    def _():
        for u in range(4):
            greet(y, u, x, core)
            greet(u, y, x, core)
            greet(u, y, x, other)

    for dx, dy in NEAR:
        greet((x + dx) % 4, (y + dy) % 4, z, core)
        greet((x + dx) % 4, (y + dy) % 4, z, other)
    greet(x, y, z, other)

    leaf_pack[...] = jnp.concatenate([rhs_half[1], rhs_half[2]], axis=1).astype(BF16)
    bias_pack[...] = jnp.concatenate([rhs_half[0], rhs_root[...]], axis=1)
    pl.semaphore_wait(barrier, 31 + 9)

    leaf_here = jnp.logical_and(x == z, x == y)
    for dz in (2, 1, 3):
        send(
            leaf_pack,
            leaf_recv.at[y],
            misc_send.at[0],
            misc_recv.at[0],
            ((z + dz) % 4, 4 * z + x, core),
        )
    send_or_keep(
        leaf_here, leaf_pack, leaf_recv.at[y], misc_self.at[0], misc_recv.at[0], (z, 4 * z + x, core)
    )
    bias_here = x == y
    for dq in (2, 1, 3):
        q = (x + dq) % 4
        send(
            bias_pack.at[pl.ds(pl.multiple_of(16 * q, 16), 16)],
            bias_recv.at[y],
            misc_send.at[1],
            misc_recv.at[1],
            (z, 4 * q + x, core),
        )
    own_rows = pl.ds(pl.multiple_of(16 * x, 16), 16)
    send_or_keep(
        bias_here,
        bias_pack.at[own_rows],
        bias_recv.at[y],
        misc_self.at[1],
        misc_recv.at[1],
        (z, 4 * x + x, core),
    )

    def scatter(src, dst, stage):
        for dx, dy in NEAR:
            peer = 4 * ((x + dx) % 4) + (y + dy) % 4
            send(
                src.at[peer],
                dst.at[col],
                scatter_send.at[stage],
                scatter_recv.at[stage],
                (z, peer, core),
            )
        start_local(src.at[col], dst.at[col], scatter_recv.at[stage])

    def spread(src, dst, stage):
        for dz in (2, 1, 3):
            send(
                src,
                dst.at[x],
                spread_send.at[stage],
                spread_recv.at[stage],
                ((z + dz) % 4, 4 * z + y, core),
            )
        send_or_keep(
            x == z,
            src,
            dst.at[x],
            spread_self.at[stage],
            spread_recv.at[stage],
            (z, 4 * z + y, core),
        )

    def spread_both(src, dst, stage):
        for dz in (2, 1, 3):
            for to in (other, core):
                send(
                    src,
                    dst.at[core, x],
                    spread_send.at[stage],
                    spread_recv.at[stage],
                    ((z + dz) % 4, 4 * z + y, to),
                )
        send(
            src,
            dst.at[core, x],
            spread_send.at[stage],
            spread_recv.at[stage],
            (z, 4 * z + y, other),
        )
        send_or_keep(
            x == z,
            src,
            dst.at[core, x],
            spread_self.at[stage],
            spread_recv.at[stage],
            (z, 4 * z + y, core),
        )

    def mask(tiles, pattern):
        @pl.loop(0, 5)
        def _(p):
            for a in range(2):
                for b in range(8):
                    here = (p, pl.ds(128 * a, 128), pl.ds(128 * b, 128))
                    keep = jnp.full((128, 128), pattern[p, a, b].astype(F32), F32)
                    tiles[here] = tiles[here] * keep.astype(BF16)

    def block(ref, j):
        return ref[:, 256 * j : 256 * j + 256]

    def chunks(ref, j, value):
        for q in range(4):
            ref[4 * q + j] = value[16 * q : 16 * q + 16].astype(BF16)

    wait_for(lower, weight_sem.at[1])
    mask(lower, lower_pattern)

    wait_for(leaf_recv, misc_recv.at[0])
    wait_for(lower_inverse, weight_sem.at[0])
    pieces = [leaf_recv[u].astype(F32) for u in range(4)]
    for s in range(2):
        leaf = jnp.concatenate([p[:, 64 * s : 64 * s + 64] for p in pieces], axis=1).astype(BF16)
        for j in range(4):
            value = dot(leaf, block(lower_inverse.at[1 + s], j))
            for q in range(4):
                send1[4 * q + j, s] = value[16 * q : 16 * q + 16].astype(BF16)
    scatter(send1, recv1, 0)
    wait_for(recv1, scatter_recv.at[0])
    leaf_value[...] = add_up(recv1, 16)
    part1[...] = leaf_value[...].astype(BF16)
    spread(part1, vec1, 0)

    wait_for(vec1, spread_recv.at[0])
    leaf1 = vec1[:, 0].reshape(64, 256)
    leaf2 = vec1[:, 1].reshape(64, 256)
    for j in range(4):
        chunks(send2, j, dot(leaf1, block(lower.at[0], j)) + dot(leaf2, block(lower.at[1], j)))
    scatter(send2, recv2, 1)
    for j in range(4):
        root_early[:, 256 * j : 256 * j + 256] = dot(leaf1, block(lower.at[3], j)) + dot(
            leaf2, block(lower.at[4], j)
        )
    wait_for(bias_recv, misc_recv.at[1])
    top_bias = jnp.concatenate([bias_recv[u][:, 0:64] for u in range(4)], axis=1)
    wait_for(recv2, scatter_recv.at[1])
    part2[...] = (top_bias - add_up(recv2, 16)).astype(BF16)
    spread(part2, vec2, 1)

    wait_for(vec2, spread_recv.at[1])
    vector = vec2[...].reshape(64, 256)
    for j in range(4):
        chunks(send3, j, dot(vector, block(lower_inverse.at[0], j)))
    scatter(send3, recv3, 2)
    wait_for(recv3, scatter_recv.at[2])
    top_value[...] = add_up(recv3, 16)
    part3[...] = top_value[...].astype(BF16)
    spread(part3, vec3, 2)

    wait_for(vec3, spread_recv.at[2])
    vector = vec3[...].reshape(64, 256)
    for j in range(4):
        value = root_early[:, 256 * j : 256 * j + 256] + dot(vector, block(lower.at[2], j))
        for half in range(2):
            for q in range(4):
                send4[half, 4 * q + j] = value[
                    16 * q : 16 * q + 16, 128 * half : 128 * half + 128
                ].astype(BF16)
    for dx, dy in NEAR:
        peer = 4 * ((x + dx) % 4) + (y + dy) % 4
        for to in (other, core):
            send(
                send4.at[to, peer],
                recv4.at[core, col],
                scatter_send.at[3],
                scatter_recv.at[3],
                (z, peer, to),
            )
    send(
        send4.at[other, col],
        recv4.at[core, col],
        scatter_send.at[3],
        scatter_recv.at[3],
        (z, col, other),
    )
    start_local(send4.at[core, col], recv4.at[core, col], scatter_recv.at[3])
    root_bias = jnp.concatenate(
        [bias_recv[2 * core][:, 64:128], bias_recv[2 * core + 1][:, 64:128]], axis=1
    )
    wait_for(upper, weight_sem.at[4])
    mask(upper, upper_pattern)
    wait_for(recv4, scatter_recv.at[3])
    part4[...] = (root_bias - add_up(recv4.at[0], 16) - add_up(recv4.at[1], 16)).astype(BF16)
    spread_both(part4, vec4, 3)

    def whole(ref):
        return jnp.concatenate([ref[0].reshape(64, 128), ref[1].reshape(64, 128)], axis=1)

    def halves(ref, vector, tiles):
        for pair in range(2):
            value = dot(vector, tiles[:, 256 * pair : 256 * pair + 256])
            for k in range(2):
                for q in range(4):
                    ref[4 * q + 2 * pair + k] = value[
                        16 * q : 16 * q + 16, 128 * k : 128 * k + 128
                    ].astype(BF16)

    wait_for(root_lower, weight_sem.at[2])
    wait_for(vec4, spread_recv.at[3])
    halves(send5, whole(vec4), root_lower)
    scatter(send5, recv5, 4)
    wait_for(recv5, scatter_recv.at[4])
    part5[...] = add_up(recv5, 16).astype(BF16)
    spread_both(part5, vec5, 4)
    wait_for(root_upper, weight_sem.at[3])
    wait_for(vec5, spread_recv.at[4])
    halves(send6, whole(vec5), root_upper)
    scatter(send6, recv6, 5)
    wait_for(recv6, scatter_recv.at[5])
    root_out[...] = add_up(recv6, 16)
    part6[...] = root_out[...].astype(BF16)
    spread_both(part6, vec6, 5)

    def out_here(k, to):
        return jnp.logical_and(jnp.logical_and(x == y, 2 * core + k == y), to == core)

    for k in range(2):
        owner = 4 * y + 2 * core + k
        send(root_out, root_out_recv.at[x], misc_send.at[2], misc_recv.at[2], (z, owner, other))
        send_or_keep(
            out_here(k, core),
            root_out,
            root_out_recv.at[x],
            misc_self.at[2 + k],
            misc_recv.at[2],
            (z, owner, core),
        )

    wait_for(vec6, spread_recv.at[5])
    vector = whole(vec6)
    for j in range(4):
        chunks(send7, j, dot(vector, block(upper.at[2], j)))
    scatter(send7, recv7, 6)
    for s in range(2):
        for j in range(4):
            second_early[s, :, 256 * j : 256 * j + 256] = dot(vector, block(upper.at[3 + s], j))
    wait_for(recv7, scatter_recv.at[6])
    part7[...] = (top_value[...] - add_up(recv7, 16)).astype(BF16)
    spread(part7, vec7, 6)

    wait_for(upper_inverse, weight_sem.at[5])
    wait_for(vec7, spread_recv.at[6])
    vector = vec7[...].reshape(64, 256)
    for j in range(4):
        chunks(send8, j, dot(vector, block(upper_inverse.at[0], j)))
    scatter(send8, recv8, 7)
    wait_for(recv8, scatter_recv.at[7])
    first = add_up(recv8, 16)
    part8[...] = first.astype(BF16)
    spread(part8, vec8, 7)
    first_out[0] = first[:, 0:128]
    first_out[1] = first[:, 128:256]
    first_here = x == y
    for du in (2, 1, 3):
        u = (y + du) % 4
        send(
            first_out.at[u // 2],
            first_out_recv.at[x],
            misc_send.at[3],
            misc_recv.at[3],
            (z, 4 * y + u, core),
        )
    send_or_keep(
        first_here,
        first_out.at[y // 2],
        first_out_recv.at[x],
        misc_self.at[4],
        misc_recv.at[3],
        (z, 4 * y + y, core),
    )

    wait_for(vec8, spread_recv.at[7])
    vector = vec8[...].reshape(64, 256)
    for s in range(2):
        for j in range(4):
            value = second_early[s, :, 256 * j : 256 * j + 256] + dot(
                vector, block(upper.at[s], j)
            )
            for q in range(4):
                send9[4 * q + j, s] = value[16 * q : 16 * q + 16].astype(BF16)
    scatter(send9, recv9, 8)

    odd = y % 2 == 1
    wait_for(root_out_recv, misc_recv.at[2])
    value = root_out_recv[...].reshape(64, 128)
    sol_root[...] = jnp.where(odd, value[:, 64:128], value[:, 0:64])
    wait_for(first_out_recv, misc_recv.at[3])
    value = first_out_recv[...].reshape(64, 128)
    sol_half[0] = jnp.where(odd, value[:, 64:128], value[:, 0:64])

    wait_for(recv9, scatter_recv.at[8])
    part9[...] = (leaf_value[...] - add_up(recv9, 16)).astype(BF16)
    spread(part9, vec9, 8)

    wait_for(vec9, spread_recv.at[8])
    second1 = vec9[:, 0].reshape(64, 256)
    second2 = vec9[:, 1].reshape(64, 256)
    for j in range(4):
        value1 = dot(second1, block(upper_inverse.at[1], j))
        value2 = dot(second2, block(upper_inverse.at[2], j))
        for u in range(4):
            span = slice(64 * u, 64 * u + 64)
            send10[4 * j + u] = jnp.concatenate([value1[:, span], value2[:, span]], axis=1).astype(
                BF16
            )
    scatter(send10, recv10, 9)
    wait_for(recv10, scatter_recv.at[9])
    total = add_up(recv10, 16)
    sol_half[1] = total[:, 0:64]
    sol_half[2] = total[:, 64:128]

    sends = (send1, send2, send3, None, send5, send6, send7, send8, send9, send10)
    for stage, ref in enumerate(sends):
        if ref is not None:
            wait_for(ref.at[pl.ds(0, 15)], scatter_send.at[stage])
    wait_for(recv4.at[0], scatter_send.at[3])
    wait_for(recv4.at[1, pl.ds(0, 15)], scatter_send.at[3])
    for stage, ref in enumerate((vec1, vec2, vec3, None, None, None, vec7, vec8, vec9)):
        if ref is not None:
            wait_for(ref.at[pl.ds(0, 3)], spread_send.at[stage])
            wait_sent_unless(x == z, ref.at[0], spread_self.at[stage])
    for stage, ref in ((3, vec4), (4, vec5), (5, vec6)):
        wait_for(ref.at[0], spread_send.at[stage])
        wait_for(ref.at[1, pl.ds(0, 3)], spread_send.at[stage])
        wait_sent_unless(x == z, ref.at[0, 0], spread_self.at[stage])
    wait_for(leaf_recv.at[pl.ds(0, 3)], misc_send.at[0])
    wait_sent_unless(leaf_here, leaf_recv.at[0], misc_self.at[0])
    wait_for(bias_recv.at[pl.ds(0, 3)], misc_send.at[1])
    wait_sent_unless(bias_here, bias_recv.at[0], misc_self.at[1])
    wait_for(root_out_recv.at[pl.ds(0, 2)], misc_send.at[2])
    for k in range(2):
        wait_sent_unless(out_here(k, core), root_out_recv.at[0], misc_self.at[2 + k])
    wait_for(first_out_recv.at[pl.ds(0, 3)], misc_send.at[3])
    wait_sent_unless(first_here, first_out_recv.at[0], misc_self.at[4])


def per_device(
    rhs_half,
    rhs_root,
    lower_coupling,
    lower_pattern,
    upper_coupling,
    upper_pattern,
    lower_inverse,
    upper_inverse,
    root_lower_inverse,
    root_upper_inverse,
):
    vmem = pl.BlockSpec(memory_space=pltpu.VMEM)
    smem = pl.BlockSpec(memory_space=pltpu.SMEM)
    hbm = pl.BlockSpec(memory_space=pl.ANY)
    one = (16, 256)
    two = (2, 16, 256)
    half = (16, 128)
    stage_chunks = [two, one, one, None, half, half, one, one, two, (64, 128)]
    exchange = [
        pltpu.VMEM((2, 16) + half if chunk is None else (16,) + chunk, BF16)
        for chunk in stage_chunks
    ]
    part_chunks = [two, one, one, half, half, half, one, one, two]
    parts = [pltpu.VMEM(chunk, BF16) for chunk in part_chunks]
    vectors = [
        pltpu.VMEM((2, 4) + chunk if chunk == half else (4,) + chunk, BF16)
        for chunk in part_chunks
    ]
    scratch = [
        pltpu.VMEM((5, 256, 1024), BF16),
        pltpu.VMEM((5, 256, 1024), BF16),
        pltpu.VMEM((3, 256, 1024), BF16),
        pltpu.VMEM((3, 256, 1024), BF16),
        pltpu.VMEM((256, 512), BF16),
        pltpu.VMEM((256, 512), BF16),
        pltpu.VMEM((64, 128), BF16),
        pltpu.VMEM((4, 64, 128), BF16),
        pltpu.VMEM((64, 128), F32),
        pltpu.VMEM((4, 16, 128), F32),
        *exchange,
        *exchange,
        *parts,
        *vectors,
        pltpu.VMEM(two, F32),
        pltpu.VMEM(one, F32),
        pltpu.VMEM((64, 1024), F32),
        pltpu.VMEM((2, 64, 1024), F32),
        pltpu.VMEM(half, F32),
        pltpu.VMEM((4,) + half, F32),
        pltpu.VMEM((2,) + half, F32),
        pltpu.VMEM((4,) + half, F32),
        pltpu.SemaphoreType.DMA((6,)),
        pltpu.SemaphoreType.DMA((10,)),
        pltpu.SemaphoreType.DMA((10,)),
        pltpu.SemaphoreType.DMA((9,)),
        pltpu.SemaphoreType.DMA((9,)),
        pltpu.SemaphoreType.DMA((9,)),
        pltpu.SemaphoreType.DMA((4,)),
        pltpu.SemaphoreType.DMA((4,)),
        pltpu.SemaphoreType.DMA((5,)),
    ]
    sol_half, sol_root = pl.pallas_call(
        kernel,
        name="tree_solve",
        out_shape=(
            jax.ShapeDtypeStruct((3, 64, 64), F32),
            jax.ShapeDtypeStruct((64, 64), F32),
        ),
        in_specs=[vmem, vmem, smem, smem] + [hbm] * 6,
        out_specs=(vmem, vmem),
        scratch_shapes=scratch,
        compiler_params=pltpu.CompilerParams(collective_id=0, has_side_effects=True),
    )(
        rhs_half[0],
        rhs_root,
        lower_pattern[0],
        upper_pattern[0],
        lower_coupling[0],
        upper_coupling[0],
        lower_inverse[0],
        upper_inverse[0],
        root_lower_inverse,
        root_upper_inverse,
    )
    return (sol_half[None], sol_root)


def solution(mesh):
    in_specs = (
        P("gz", None, None, ("row", "col")),
        P(None, ("row", "col")),
        P("gz", None, "col", "row"),
        P("gz", None, "col", "row"),
        P("gz", None, "col", "row"),
        P("gz", None, "col", "row"),
        P("gz", None, "col", "row"),
        P("gz", None, "col", "row"),
        P("col", "row"),
        P("col", "row"),
    )
    out_specs = (P("gz", None, None, ("row", "col")), P(None, ("row", "col")))
    return jax.shard_map(
        per_device, mesh=mesh, in_specs=in_specs, out_specs=out_specs, check_vma=False
    )
```

time: 1070 us -> 113 us (0.11)
  waiting for transfers between devices: 526 us -> 0 us
  blocking collectives: 473 us -> 0 us
  Pallas kernels: 0 us -> 109 us
  local copies, waits for them, and re-layouts: 33.8 us -> 2.91 us
  between operations: 14.2 us -> 0.64 us
  matrix products: 13.1 us -> 0 us
  other arithmetic: 11 us -> 0 us
    psum x6 -> x0, waiting for transfers between devices: 415 us -> none  [the longest x5 395 us: settle(): summed = lax.psum(partial_value, 'col')]
    psum x5 -> x0, blocking collectives: 380 us -> none  [settle(): summed = lax.psum(partial_value, 'col')]
    all_gather x3 -> x0, waiting for transfers between devices: 110 us -> none  [the longest x1 70.3 us: per_device(): lax.all_gather(rhs_half[0, 1:3].astype(jnp.bfloat16), ('row', 'col'), axi...]
    pallas_call x0 -> x1, Pallas kernels: none -> 109 us  [per_device(): pl.pallas_call(kernel, name='tree_solve', out_shape=(jax.ShapeDtypeStruct...]
    all_gather x7 -> x0, blocking collectives: 93.3 us -> none  [settle(): lax.all_gather(summed.astype(jnp.bfloat16), 'row', axis=2, tiled=True)]
    slice x11 -> x0, local copies, waits for them, and re-layouts: 13.4 us -> none  [the longest x2 3.8 us: per_device(): root_terms = -multiply(every_cols, lower[2:5]).sum(axis=0, keepdims=True)]
    dot_general x11 -> x0, matrix products: 13.1 us -> none  [the longest x8 9.67 us: multiply(): jnp.einsum('snj,sji->sni', vectors, tiles, preferred_element_type=jnp.flo...]
  transfers between devices with their start and end apart: 9 -> 0, of which waited for: 9 -> 0; matrix products, arithmetic and copies ran while one was open for 2% -> 0% of each run, Pallas kernels for 0% -> 0%
where the time goes in v1:
time: 113 us
  Pallas kernels  109 us (96%)
  local copies, waits for them, and re-layouts  2.91 us (3%)
    pallas_call x1, Pallas kernels, per_device(): pl.pallas_call(kernel, name='tree_solve', out_shape=(jax.ShapeDtypeStruct...  109 us
    unnamed x2, local copies, waits for them, and re-layouts  2.91 us

profile of v1, /device:TPU:0, one launch (start us, length us, event | category | flops | bytes accessed | tf_op | source)
XLA Modules:
  0.0 112.9 jit_solution(8321578016534031029)
XLA Ops:
  0.6 109.3 %tree_solve.1 = (f32[3,64,64]{2,1,0:T(8,128)}, f32[64,64]{1,0:T(8,128)}) custom-call(f32[3,64,64]{2,1,0:T(8,128)} %bitcast.12, f32[64,64]{1,0:T(8,128)} %rhs_root.1, s32[5,2,8]{2,1,0:T(2,128)} %bitcast.14, s32[5,2,8]{2,1,0:T(2,128)} %bitcast.15, bf16[5,256,1024]{2,1,0:T(8,128)(2,1)} %bitcast.8, bf16[5,256,1024]{2,1,0:T(8,128)(2,1)} %bitcast.9, ...), custom_call_target="tpu_custom_call" | custom-call | tf_op jit(solution)/shard_map/tree_solve/pallas_call | solution.py:580
  110.0 1.5 %copy.14 = f32[1,3,64,64]{3,2,1,0:T(8,128)} copy(f32[1,3,64,64]{3,2,1,0:T(8,128)} %bitcast.13) | data formatting | bytes 98304
  111.5 1.4 %copy.15 = f32[64,64]{1,0:T(8,128)} copy(f32[64,64]{1,0:T(8,128)} %get-tuple-element.9) | data formatting | bytes 32768

commit v2 on v1

--- a/solution.py
+++ b/solution.py
@@ -27,10 +27,10 @@
 
 
 def kernel(
-    rhs_half,
-    rhs_root,
-    lower_pattern,
-    upper_pattern,
+    rhs_half_hbm,
+    rhs_root_hbm,
+    lower_pattern_hbm,
+    upper_pattern_hbm,
     lower_hbm,
     upper_hbm,
     lower_inverse_hbm,
@@ -39,6 +39,10 @@
     root_upper_hbm,
     sol_half,
     sol_root,
+    rhs_half,
+    rhs_root,
+    lower_pattern,
+    upper_pattern,
     lower,
     upper,
     lower_inverse,
@@ -142,6 +146,29 @@
         def _():
             wait_for(ref, sem)
 
+    barrier = pltpu.get_barrier_semaphore()
+
+    def greet(px, py, pz, pcore):
+        pl.semaphore_signal(
+            barrier, inc=1, device_id=(pz, 4 * px + py, pcore), device_id_type=MESH
+        )
+
+    @pl.when(x != z)
+    def _():
+        for u in range(4):
+            greet(y, u, x, core)
+            greet(u, y, x, core)
+            greet(u, y, x, other)
+
+    for dx, dy in NEAR:
+        greet((x + dx) % 4, (y + dy) % 4, z, core)
+        greet((x + dx) % 4, (y + dy) % 4, z, other)
+    greet(x, y, z, other)
+
+    start_local(rhs_half_hbm, rhs_half, weight_sem.at[6])
+    start_local(rhs_root_hbm, rhs_root, weight_sem.at[7])
+    start_local(lower_pattern_hbm, lower_pattern, weight_sem.at[8])
+    start_local(upper_pattern_hbm, upper_pattern, weight_sem.at[9])
     start_local(lower_inverse_hbm, lower_inverse, weight_sem.at[0])
     start_local(lower_hbm, lower, weight_sem.at[1])
     for j in range(4):
@@ -157,25 +184,8 @@
     start_local(upper_hbm, upper, weight_sem.at[4])
     start_local(upper_inverse_hbm, upper_inverse, weight_sem.at[5])
 
-    barrier = pltpu.get_barrier_semaphore()
-
-    def greet(px, py, pz, pcore):
-        pl.semaphore_signal(
-            barrier, inc=1, device_id=(pz, 4 * px + py, pcore), device_id_type=MESH
-        )
-
-    @pl.when(x != z)
-    def _():
-        for u in range(4):
-            greet(y, u, x, core)
-            greet(u, y, x, core)
-            greet(u, y, x, other)
-
-    for dx, dy in NEAR:
-        greet((x + dx) % 4, (y + dy) % 4, z, core)
-        greet((x + dx) % 4, (y + dy) % 4, z, other)
-    greet(x, y, z, other)
-
+    wait_for(rhs_half, weight_sem.at[6])
+    wait_for(rhs_root, weight_sem.at[7])
     leaf_pack[...] = jnp.concatenate([rhs_half[1], rhs_half[2]], axis=1).astype(BF16)
     bias_pack[...] = jnp.concatenate([rhs_half[0], rhs_root[...]], axis=1)
     pl.semaphore_wait(barrier, 31 + 9)
@@ -277,26 +287,53 @@
                     keep = jnp.full((128, 128), pattern[p, a, b].astype(F32), F32)
                     tiles[here] = tiles[here] * keep.astype(BF16)
 
+    def columns_of(j):
+        return pl.ds(pl.multiple_of(256 * j, 256), 256)
+
     def block(ref, j):
-        return ref[:, 256 * j : 256 * j + 256]
-
-    def chunks(ref, j, value):
-        for q in range(4):
-            ref[4 * q + j] = value[16 * q : 16 * q + 16].astype(BF16)
+        return ref[:, columns_of(j)]
+
+    def multiply(values_of, src, dst, stage):
+        for dy in (2, 1, 3, 0):
+            j = (y + dy) % 4
+            values = values_of(j)
+            for q in range(4):
+                rows = [value[16 * q : 16 * q + 16].astype(BF16) for value in values]
+                if len(rows) == 1:
+                    src[4 * q + j] = rows[0]
+                else:
+                    for s in range(2):
+                        src[4 * q + j, s] = rows[s]
+            for dx in (2, 1, 3, 0):
+                peer = 4 * ((x + dx) % 4) + j
+                if dx or dy:
+                    send(
+                        src.at[peer],
+                        dst.at[col],
+                        scatter_send.at[stage],
+                        scatter_recv.at[stage],
+                        (z, peer, core),
+                    )
+                else:
+                    start_local(src.at[peer], dst.at[col], scatter_recv.at[stage])
 
     wait_for(lower, weight_sem.at[1])
+    wait_for(lower_pattern, weight_sem.at[8])
     mask(lower, lower_pattern)
 
     wait_for(leaf_recv, misc_recv.at[0])
     wait_for(lower_inverse, weight_sem.at[0])
     pieces = [leaf_recv[u].astype(F32) for u in range(4)]
-    for s in range(2):
-        leaf = jnp.concatenate([p[:, 64 * s : 64 * s + 64] for p in pieces], axis=1).astype(BF16)
-        for j in range(4):
-            value = dot(leaf, block(lower_inverse.at[1 + s], j))
-            for q in range(4):
-                send1[4 * q + j, s] = value[16 * q : 16 * q + 16].astype(BF16)
-    scatter(send1, recv1, 0)
+    leaves = [
+        jnp.concatenate([p[:, 64 * s : 64 * s + 64] for p in pieces], axis=1).astype(BF16)
+        for s in range(2)
+    ]
+    multiply(
+        lambda j: [dot(leaves[s], block(lower_inverse.at[1 + s], j)) for s in range(2)],
+        send1,
+        recv1,
+        0,
+    )
     wait_for(recv1, scatter_recv.at[0])
     leaf_value[...] = add_up(recv1, 16)
     part1[...] = leaf_value[...].astype(BF16)
@@ -305,9 +342,12 @@
     wait_for(vec1, spread_recv.at[0])
     leaf1 = vec1[:, 0].reshape(64, 256)
     leaf2 = vec1[:, 1].reshape(64, 256)
-    for j in range(4):
-        chunks(send2, j, dot(leaf1, block(lower.at[0], j)) + dot(leaf2, block(lower.at[1], j)))
-    scatter(send2, recv2, 1)
+    multiply(
+        lambda j: [dot(leaf1, block(lower.at[0], j)) + dot(leaf2, block(lower.at[1], j))],
+        send2,
+        recv2,
+        1,
+    )
     for j in range(4):
         root_early[:, 256 * j : 256 * j + 256] = dot(leaf1, block(lower.at[3], j)) + dot(
             leaf2, block(lower.at[4], j)
@@ -320,9 +360,8 @@
 
     wait_for(vec2, spread_recv.at[1])
     vector = vec2[...].reshape(64, 256)
-    for j in range(4):
-        chunks(send3, j, dot(vector, block(lower_inverse.at[0], j)))
-    scatter(send3, recv3, 2)
+    vector3 = vector
+    multiply(lambda j: [dot(vector3, block(lower_inverse.at[0], j))], send3, recv3, 2)
     wait_for(recv3, scatter_recv.at[2])
     top_value[...] = add_up(recv3, 16)
     part3[...] = top_value[...].astype(BF16)
@@ -330,35 +369,32 @@
 
     wait_for(vec3, spread_recv.at[2])
     vector = vec3[...].reshape(64, 256)
-    for j in range(4):
-        value = root_early[:, 256 * j : 256 * j + 256] + dot(vector, block(lower.at[2], j))
+    for dy in (2, 1, 3, 0):
+        j = (y + dy) % 4
+        value = root_early[:, columns_of(j)] + dot(vector, block(lower.at[2], j))
         for half in range(2):
             for q in range(4):
                 send4[half, 4 * q + j] = value[
                     16 * q : 16 * q + 16, 128 * half : 128 * half + 128
                 ].astype(BF16)
-    for dx, dy in NEAR:
-        peer = 4 * ((x + dx) % 4) + (y + dy) % 4
-        for to in (other, core):
-            send(
-                send4.at[to, peer],
-                recv4.at[core, col],
-                scatter_send.at[3],
-                scatter_recv.at[3],
-                (z, peer, to),
-            )
-    send(
-        send4.at[other, col],
-        recv4.at[core, col],
-        scatter_send.at[3],
-        scatter_recv.at[3],
-        (z, col, other),
-    )
-    start_local(send4.at[core, col], recv4.at[core, col], scatter_recv.at[3])
+        for dx in (2, 1, 3, 0):
+            peer = 4 * ((x + dx) % 4) + j
+            for to in (other, core):
+                if dx or dy or to is other:
+                    send(
+                        send4.at[to, peer],
+                        recv4.at[core, col],
+                        scatter_send.at[3],
+                        scatter_recv.at[3],
+                        (z, peer, to),
+                    )
+                else:
+                    start_local(send4.at[to, peer], recv4.at[core, col], scatter_recv.at[3])
     root_bias = jnp.concatenate(
         [bias_recv[2 * core][:, 64:128], bias_recv[2 * core + 1][:, 64:128]], axis=1
     )
     wait_for(upper, weight_sem.at[4])
+    wait_for(upper_pattern, weight_sem.at[9])
     mask(upper, upper_pattern)
     wait_for(recv4, scatter_recv.at[3])
     part4[...] = (root_bias - add_up(recv4.at[0], 16) - add_up(recv4.at[1], 16)).astype(BF16)
@@ -409,9 +445,8 @@
 
     wait_for(vec6, spread_recv.at[5])
     vector = whole(vec6)
-    for j in range(4):
-        chunks(send7, j, dot(vector, block(upper.at[2], j)))
-    scatter(send7, recv7, 6)
+    vector7 = vector
+    multiply(lambda j: [dot(vector7, block(upper.at[2], j))], send7, recv7, 6)
     for s in range(2):
         for j in range(4):
             second_early[s, :, 256 * j : 256 * j + 256] = dot(vector, block(upper.at[3 + s], j))
@@ -422,9 +457,8 @@
     wait_for(upper_inverse, weight_sem.at[5])
     wait_for(vec7, spread_recv.at[6])
     vector = vec7[...].reshape(64, 256)
-    for j in range(4):
-        chunks(send8, j, dot(vector, block(upper_inverse.at[0], j)))
-    scatter(send8, recv8, 7)
+    vector8 = vector
+    multiply(lambda j: [dot(vector8, block(upper_inverse.at[0], j))], send8, recv8, 7)
     wait_for(recv8, scatter_recv.at[7])
     first = add_up(recv8, 16)
     part8[...] = first.astype(BF16)
@@ -452,14 +486,16 @@
 
     wait_for(vec8, spread_recv.at[7])
     vector = vec8[...].reshape(64, 256)
-    for s in range(2):
-        for j in range(4):
-            value = second_early[s, :, 256 * j : 256 * j + 256] + dot(
-                vector, block(upper.at[s], j)
-            )
-            for q in range(4):
-                send9[4 * q + j, s] = value[16 * q : 16 * q + 16].astype(BF16)
-    scatter(send9, recv9, 8)
+    vector9 = vector
+    multiply(
+        lambda j: [
+            second_early[s, :, columns_of(j)] + dot(vector9, block(upper.at[s], j))
+            for s in range(2)
+        ],
+        send9,
+        recv9,
+        8,
+    )
 
     odd = y % 2 == 1
     wait_for(root_out_recv, misc_recv.at[2])
@@ -476,7 +512,8 @@
     wait_for(vec9, spread_recv.at[8])
     second1 = vec9[:, 0].reshape(64, 256)
     second2 = vec9[:, 1].reshape(64, 256)
-    for j in range(4):
+    for dx in (2, 1, 3, 0):
+        j = (x + dx) % 4
         value1 = dot(second1, block(upper_inverse.at[1], j))
         value2 = dot(second2, block(upper_inverse.at[2], j))
         for u in range(4):
@@ -484,7 +521,18 @@
             send10[4 * j + u] = jnp.concatenate([value1[:, span], value2[:, span]], axis=1).astype(
                 BF16
             )
-    scatter(send10, recv10, 9)
+        for dy in (2, 1, 3, 0):
+            peer = 4 * j + (y + dy) % 4
+            if dx or dy:
+                send(
+                    send10.at[peer],
+                    recv10.at[col],
+                    scatter_send.at[9],
+                    scatter_recv.at[9],
+                    (z, peer, core),
+                )
+            else:
+                start_local(send10.at[peer], recv10.at[col], scatter_recv.at[9])
     wait_for(recv10, scatter_recv.at[9])
     total = add_up(recv10, 16)
     sol_half[1] = total[:, 0:64]
@@ -528,7 +576,6 @@
     root_upper_inverse,
 ):
     vmem = pl.BlockSpec(memory_space=pltpu.VMEM)
-    smem = pl.BlockSpec(memory_space=pltpu.SMEM)
     hbm = pl.BlockSpec(memory_space=pl.ANY)
     one = (16, 256)
     two = (2, 16, 256)
@@ -545,6 +592,10 @@
         for chunk in part_chunks
     ]
     scratch = [
+        pltpu.VMEM((3, 64, 64), F32),
+        pltpu.VMEM((64, 64), F32),
+        pltpu.SMEM((5, 2, 8), jnp.int32),
+        pltpu.SMEM((5, 2, 8), jnp.int32),
         pltpu.VMEM((5, 256, 1024), BF16),
         pltpu.VMEM((5, 256, 1024), BF16),
         pltpu.VMEM((3, 256, 1024), BF16),
@@ -567,7 +618,7 @@
         pltpu.VMEM((4,) + half, F32),
         pltpu.VMEM((2,) + half, F32),
         pltpu.VMEM((4,) + half, F32),
-        pltpu.SemaphoreType.DMA((6,)),
+        pltpu.SemaphoreType.DMA((10,)),
         pltpu.SemaphoreType.DMA((10,)),
         pltpu.SemaphoreType.DMA((10,)),
         pltpu.SemaphoreType.DMA((9,)),
@@ -580,11 +631,8 @@
     sol_half, sol_root = pl.pallas_call(
         kernel,
         name="tree_solve",
-        out_shape=(
-            jax.ShapeDtypeStruct((3, 64, 64), F32),
-            jax.ShapeDtypeStruct((64, 64), F32),
-        ),
-        in_specs=[vmem, vmem, smem, smem] + [hbm] * 6,
+        out_shape=(pltpu.VMEM((3, 64, 64), F32), pltpu.VMEM((64, 64), F32)),
+        in_specs=[hbm] * 10,
         out_specs=(vmem, vmem),
         scratch_shapes=scratch,
         compiler_params=pltpu.CompilerParams(collective_id=0, has_side_effects=True),
@@ -600,6 +648,27 @@
         root_lower_inverse,
         root_upper_inverse,
     )
+
+    def leave(half_ref, root_ref, half_out, root_out, sems):
+        first = pltpu.make_async_copy(half_ref, half_out, sems.at[0])
+        second = pltpu.make_async_copy(root_ref, root_out, sems.at[1])
+        first.start()
+        second.start()
+        first.wait()
+        second.wait()
+
+    sol_half, sol_root = pl.pallas_call(
+        leave,
+        name="leave",
+        out_shape=(
+            jax.ShapeDtypeStruct((3, 64, 64), F32),
+            jax.ShapeDtypeStruct((64, 64), F32),
+        ),
+        in_specs=[vmem, vmem],
+        out_specs=(hbm, hbm),
+        scratch_shapes=[pltpu.SemaphoreType.DMA((2,))],
+        compiler_params=pltpu.CompilerParams(vmem_limit_bytes=1 << 20),
+    )(sol_half, sol_root)
     return (sol_half[None], sol_root)
 
 

time: 113 us -> 110 us (0.973)
  local copies, waits for them, and re-layouts: 2.91 us -> 0 us
    unnamed x2 -> x0, local copies, waits for them, and re-layouts: 2.91 us -> none
    pallas_call x1 -> x2, Pallas kernels: 109 us -> 109 us  [the longest x1 108 us: per_device(): pl.pallas_call(kernel, name='tree_solve', out_shape=(pltpu.VMEM((3, 64, 6...]
where the time goes in v2:
time: 110 us; the launch traced here: 109 us
  Pallas kernels  109 us (99%)
    pallas_call x1, Pallas kernels, per_device(): pl.pallas_call(kernel, name='tree_solve', out_shape=(pltpu.VMEM((3, 64, 6...  108 us

profile of v2, /device:TPU:0, one launch (start us, length us, event | category | flops | bytes accessed | tf_op | source)
XLA Modules:
  0.0 109.4 jit_solution(6240293651257917894)
XLA Ops:
  0.6 108.1 %tree_solve.1 = (f32[3,64,64]{2,1,0:T(8,128)S(1)}, f32[64,64]{1,0:T(8,128)S(1)}) custom-call(f32[3,64,64]{2,1,0:T(8,128)} %bitcast.12, f32[64,64]{1,0:T(8,128)} %rhs_root_hbm.1, s32[5,2,8]{2,1,0:T(2,128)} %bitcast.13, s32[5,2,8]{2,1,0:T(2,128)} %bitcast.14, bf16[5,256,1024]{2,1,0:T(8,128)(2,1)} %bitcast.8, bf16[5,256,1024]{2,1,0:T(8,128)(2,1)} %bitcast.9, ...), custom_call_target="tpu_custom_call" | custom-call | tf_op jit(solution)/shard_map/tree_solve/pallas_call | solution.py:631
  108.8 0.7 leave.1

commit v3 on v2

--- a/solution.py
+++ b/solution.py
@@ -51,6 +51,7 @@
     root_upper,
     leaf_pack,
     leaf_recv,
+    leaf_relay,
     bias_pack,
     bias_recv,
     send1,
@@ -108,6 +109,9 @@
     misc_send,
     misc_recv,
     misc_self,
+    relay_sem,
+    ready,
+    go,
 ):
     z = lax.axis_index("row")
     col = lax.axis_index("col")
@@ -153,17 +157,25 @@
             barrier, inc=1, device_id=(pz, 4 * px + py, pcore), device_id_type=MESH
         )
 
-    @pl.when(x != z)
+    @pl.when(core == 0)
     def _():
         for u in range(4):
-            greet(y, u, x, core)
-            greet(u, y, x, core)
-            greet(u, y, x, other)
-
-    for dx, dy in NEAR:
-        greet((x + dx) % 4, (y + dy) % 4, z, core)
-        greet((x + dx) % 4, (y + dy) % 4, z, other)
-    greet(x, y, z, other)
+            greet(y, u, x, 1)
+        for dz in (2, 1, 3):
+            greet(z, y, (z + dz) % 4, 0)
+
+        @pl.when(x != z)
+        def _():
+            for u in range(4):
+                greet(y, u, x, 0)
+                greet(u, y, x, 0)
+
+        for dx, dy in NEAR:
+            greet((x + dx) % 4, (y + dy) % 4, z, 0)
+
+    @pl.when(core == 1)
+    def _():
+        greet(x, y, z, 0)
 
     start_local(rhs_half_hbm, rhs_half, weight_sem.at[6])
     start_local(rhs_root_hbm, rhs_root, weight_sem.at[7])
@@ -188,39 +200,60 @@
     wait_for(rhs_root, weight_sem.at[7])
     leaf_pack[...] = jnp.concatenate([rhs_half[1], rhs_half[2]], axis=1).astype(BF16)
     bias_pack[...] = jnp.concatenate([rhs_half[0], rhs_root[...]], axis=1)
-    pl.semaphore_wait(barrier, 31 + 9)
+
+    def tell(px, py, pz):
+        pl.semaphore_signal(ready, inc=1, device_id=(pz, 4 * px + py, 0), device_id_type=MESH)
+
+    @pl.when(core == 0)
+    def _():
+        @pl.when(x == z)
+        def _():
+            pl.semaphore_wait(barrier, 15 + 3 + 3 + 1)
+
+        @pl.when(x != z)
+        def _():
+            pl.semaphore_wait(barrier, 15 + 3 + 3 + 1 + 4)
+            for u in range(4):
+                tell(u, y, x)
+
+        for dx, dy in NEAR:
+            tell((x + dx) % 4, (y + dy) % 4, z)
+
+    @pl.when(core == 1)
+    def _():
+        pl.semaphore_wait(barrier, 4)
 
     leaf_here = jnp.logical_and(x == z, x == y)
-    for dz in (2, 1, 3):
-        send(
+
+    @pl.when(core == 0)
+    def _():
+        for dz in (2, 1, 3):
+            send(
+                leaf_pack,
+                leaf_recv.at[y],
+                misc_send.at[0],
+                misc_recv.at[0],
+                ((z + dz) % 4, 4 * z + x, 0),
+            )
+        send_or_keep(
+            leaf_here,
             leaf_pack,
             leaf_recv.at[y],
-            misc_send.at[0],
+            misc_self.at[0],
             misc_recv.at[0],
-            ((z + dz) % 4, 4 * z + x, core),
-        )
-    send_or_keep(
-        leaf_here, leaf_pack, leaf_recv.at[y], misc_self.at[0], misc_recv.at[0], (z, 4 * z + x, core)
-    )
-    bias_here = x == y
-    for dq in (2, 1, 3):
-        q = (x + dq) % 4
-        send(
-            bias_pack.at[pl.ds(pl.multiple_of(16 * q, 16), 16)],
-            bias_recv.at[y],
-            misc_send.at[1],
-            misc_recv.at[1],
-            (z, 4 * q + x, core),
-        )
-    own_rows = pl.ds(pl.multiple_of(16 * x, 16), 16)
-    send_or_keep(
-        bias_here,
-        bias_pack.at[own_rows],
-        bias_recv.at[y],
-        misc_self.at[1],
-        misc_recv.at[1],
-        (z, 4 * x + x, core),
-    )
+            (z, 4 * z + x, 0),
+        )
+
+    @pl.when(core == 1)
+    def _():
+        for dz in (2, 1, 3, 0):
+            send(
+                leaf_pack,
+                leaf_relay.at[y],
+                misc_send.at[0],
+                relay_sem.at[0],
+                ((z + dz) % 4, 4 * z + x, 0),
+            )
 
     def scatter(src, dst, stage):
         for dx, dy in NEAR:
@@ -320,6 +353,40 @@
     wait_for(lower, weight_sem.at[1])
     wait_for(lower_pattern, weight_sem.at[8])
     mask(lower, lower_pattern)
+
+    @pl.when(core == 0)
+    def _():
+        pl.semaphore_wait(ready, 15 + 3)
+        pl.semaphore_signal(go, inc=1, device_id=(z, col, 1), device_id_type=MESH)
+
+    @pl.when(core == 1)
+    def _():
+        pl.semaphore_wait(go, 1)
+
+    bias_here = x == y
+    for dq in (2, 1, 3):
+        q = (x + dq) % 4
+        send(
+            bias_pack.at[pl.ds(pl.multiple_of(16 * q, 16), 16)],
+            bias_recv.at[y],
+            misc_send.at[1],
+            misc_recv.at[1],
+            (z, 4 * q + x, core),
+        )
+    own_rows = pl.ds(pl.multiple_of(16 * x, 16), 16)
+    send_or_keep(
+        bias_here,
+        bias_pack.at[own_rows],
+        bias_recv.at[y],
+        misc_self.at[1],
+        misc_recv.at[1],
+        (z, 4 * x + x, core),
+    )
+
+    @pl.when(core == 0)
+    def _():
+        wait_for(leaf_relay, relay_sem.at[0])
+        send(leaf_relay, leaf_recv, relay_sem.at[1], misc_recv.at[0], (z, col, 1))
 
     wait_for(leaf_recv, misc_recv.at[0])
     wait_for(lower_inverse, weight_sem.at[0])
@@ -553,7 +620,16 @@
         wait_for(ref.at[1, pl.ds(0, 3)], spread_send.at[stage])
         wait_sent_unless(x == z, ref.at[0, 0], spread_self.at[stage])
     wait_for(leaf_recv.at[pl.ds(0, 3)], misc_send.at[0])
-    wait_sent_unless(leaf_here, leaf_recv.at[0], misc_self.at[0])
+
+    @pl.when(core == 0)
+    def _():
+        wait_for(leaf_recv, relay_sem.at[1])
+        wait_sent_unless(leaf_here, leaf_recv.at[0], misc_self.at[0])
+
+    @pl.when(core == 1)
+    def _():
+        wait_for(leaf_recv.at[0], misc_send.at[0])
+
     wait_for(bias_recv.at[pl.ds(0, 3)], misc_send.at[1])
     wait_sent_unless(bias_here, bias_recv.at[0], misc_self.at[1])
     wait_for(root_out_recv.at[pl.ds(0, 2)], misc_send.at[2])
@@ -604,6 +680,7 @@
         pltpu.VMEM((256, 512), BF16),
         pltpu.VMEM((64, 128), BF16),
         pltpu.VMEM((4, 64, 128), BF16),
+        pltpu.VMEM((4, 64, 128), BF16),
         pltpu.VMEM((64, 128), F32),
         pltpu.VMEM((4, 16, 128), F32),
         *exchange,
@@ -627,6 +704,9 @@
         pltpu.SemaphoreType.DMA((4,)),
         pltpu.SemaphoreType.DMA((4,)),
         pltpu.SemaphoreType.DMA((5,)),
+        pltpu.SemaphoreType.DMA((2,)),
+        pltpu.SemaphoreType.REGULAR,
+        pltpu.SemaphoreType.REGULAR,
     ]
     sol_half, sol_root = pl.pallas_call(
         kernel,

time: 110 us -> 109 us (level)
  no operation moved by 1% of the time
where the time goes in v3:
time: 109 us
  Pallas kernels  109 us (100%)
    pallas_call x1, Pallas kernels, per_device(): pl.pallas_call(kernel, name='tree_solve', out_shape=(pltpu.VMEM((3, 64, 6...  108 us

profile of v3, /device:TPU:0, one launch (start us, length us, event | category | flops | bytes accessed | tf_op | source)
XLA Modules:
  0.0 109.4 jit_solution(17427385460677137348)
XLA Ops:
  0.6 108.1 %tree_solve.1 = (f32[3,64,64]{2,1,0:T(8,128)S(1)}, f32[64,64]{1,0:T(8,128)S(1)}) custom-call(f32[3,64,64]{2,1,0:T(8,128)} %bitcast.12, f32[64,64]{1,0:T(8,128)} %rhs_root_hbm.1, s32[5,2,8]{2,1,0:T(2,128)} %bitcast.13, s32[5,2,8]{2,1,0:T(2,128)} %bitcast.14, bf16[5,256,1024]{2,1,0:T(8,128)(2,1)} %bitcast.8, bf16[5,256,1024]{2,1,0:T(8,128)(2,1)} %bitcast.9, ...), custom_call_target="tpu_custom_call" | custom-call | tf_op jit(solution)/shard_map/tree_solve/pallas_call | solution.py:711
  108.7 0.7 leave.1

commit v4 on v3

--- a/solution.py
+++ b/solution.py
@@ -110,6 +110,7 @@
     misc_recv,
     misc_self,
     relay_sem,
+    here,
     ready,
     go,
 ):
@@ -159,6 +160,7 @@
 
     @pl.when(core == 0)
     def _():
+        greet(x, y, z, 1)
         for u in range(4):
             greet(y, u, x, 1)
         for dz in (2, 1, 3):
@@ -173,55 +175,27 @@
         for dx, dy in NEAR:
             greet((x + dx) % 4, (y + dy) % 4, z, 0)
 
-    @pl.when(core == 1)
-    def _():
-        greet(x, y, z, 0)
-
     start_local(rhs_half_hbm, rhs_half, weight_sem.at[6])
     start_local(rhs_root_hbm, rhs_root, weight_sem.at[7])
-    start_local(lower_pattern_hbm, lower_pattern, weight_sem.at[8])
-    start_local(upper_pattern_hbm, upper_pattern, weight_sem.at[9])
-    start_local(lower_inverse_hbm, lower_inverse, weight_sem.at[0])
-    start_local(lower_hbm, lower, weight_sem.at[1])
-    for j in range(4):
-        columns = pl.ds(pl.multiple_of(256 * j + 128 * core, 128), 128)
-        start_local(
-            root_lower_hbm.at[:, columns], root_lower.at[:, pl.ds(128 * j, 128)], weight_sem.at[2]
-        )
-    for j in range(4):
-        columns = pl.ds(pl.multiple_of(256 * j + 128 * core, 128), 128)
-        start_local(
-            root_upper_hbm.at[:, columns], root_upper.at[:, pl.ds(128 * j, 128)], weight_sem.at[3]
-        )
-    start_local(upper_hbm, upper, weight_sem.at[4])
-    start_local(upper_inverse_hbm, upper_inverse, weight_sem.at[5])
-
     wait_for(rhs_half, weight_sem.at[6])
     wait_for(rhs_root, weight_sem.at[7])
     leaf_pack[...] = jnp.concatenate([rhs_half[1], rhs_half[2]], axis=1).astype(BF16)
     bias_pack[...] = jnp.concatenate([rhs_half[0], rhs_root[...]], axis=1)
 
-    def tell(px, py, pz):
-        pl.semaphore_signal(ready, inc=1, device_id=(pz, 4 * px + py, 0), device_id_type=MESH)
-
     @pl.when(core == 0)
     def _():
         @pl.when(x == z)
         def _():
-            pl.semaphore_wait(barrier, 15 + 3 + 3 + 1)
+            pl.semaphore_wait(barrier, 15 + 3 + 3)
 
         @pl.when(x != z)
         def _():
-            pl.semaphore_wait(barrier, 15 + 3 + 3 + 1 + 4)
-            for u in range(4):
-                tell(u, y, x)
-
-        for dx, dy in NEAR:
-            tell((x + dx) % 4, (y + dy) % 4, z)
+            pl.semaphore_wait(barrier, 15 + 3 + 3 + 4)
 
     @pl.when(core == 1)
     def _():
-        pl.semaphore_wait(barrier, 4)
+        pl.semaphore_wait(barrier, 1 + 4)
+        pl.semaphore_signal(here, inc=1, device_id=(z, col, 0), device_id_type=MESH)
 
     leaf_here = jnp.logical_and(x == z, x == y)
 
@@ -251,9 +225,27 @@
                 leaf_pack,
                 leaf_relay.at[y],
                 misc_send.at[0],
-                relay_sem.at[0],
+                relay_sem.at[y],
                 ((z + dz) % 4, 4 * z + x, 0),
             )
+
+    start_local(lower_pattern_hbm, lower_pattern, weight_sem.at[8])
+    start_local(upper_pattern_hbm, upper_pattern, weight_sem.at[9])
+    start_local(lower_inverse_hbm, lower_inverse, weight_sem.at[0])
+    start_local(lower_hbm, lower, weight_sem.at[1])
+    for j in range(4):
+        columns = pl.ds(pl.multiple_of(256 * j + 128 * core, 128), 128)
+        start_local(
+            root_lower_hbm.at[:, columns], root_lower.at[:, pl.ds(128 * j, 128)], weight_sem.at[2]
+        )
+    for j in range(4):
+        columns = pl.ds(pl.multiple_of(256 * j + 128 * core, 128), 128)
+        start_local(
+            root_upper_hbm.at[:, columns], root_upper.at[:, pl.ds(128 * j, 128)], weight_sem.at[3]
+        )
+    start_local(upper_hbm, upper, weight_sem.at[4])
+    start_local(upper_inverse_hbm, upper_inverse, weight_sem.at[5])
+
 
     def scatter(src, dst, stage):
         for dx, dy in NEAR:
@@ -350,43 +342,52 @@
                 else:
                     start_local(src.at[peer], dst.at[col], scatter_recv.at[stage])
 
+    bias_here = x == y
+
+    def send_biases():
+        for dq in (2, 1, 3):
+            q = (x + dq) % 4
+            send(
+                bias_pack.at[pl.ds(pl.multiple_of(16 * q, 16), 16)],
+                bias_recv.at[y],
+                misc_send.at[1],
+                misc_recv.at[1],
+                (z, 4 * q + x, core),
+            )
+        own_rows = pl.ds(pl.multiple_of(16 * x, 16), 16)
+        send_or_keep(
+            bias_here,
+            bias_pack.at[own_rows],
+            bias_recv.at[y],
+            misc_self.at[1],
+            misc_recv.at[1],
+            (z, 4 * x + x, core),
+        )
+
+    def tell(px, py, pz):
+        pl.semaphore_signal(ready, inc=1, device_id=(pz, 4 * px + py, 0), device_id_type=MESH)
+
+    @pl.when(core == 0)
+    def _():
+        send_biases()
+        pl.semaphore_wait(here, 1)
+
+        @pl.when(x != z)
+        def _():
+            for u in range(4):
+                tell(u, y, x)
+
+        for dx, dy in NEAR:
+            tell((x + dx) % 4, (y + dy) % 4, z)
+
     wait_for(lower, weight_sem.at[1])
     wait_for(lower_pattern, weight_sem.at[8])
     mask(lower, lower_pattern)
 
-    @pl.when(core == 0)
-    def _():
-        pl.semaphore_wait(ready, 15 + 3)
-        pl.semaphore_signal(go, inc=1, device_id=(z, col, 1), device_id_type=MESH)
-
     @pl.when(core == 1)
     def _():
         pl.semaphore_wait(go, 1)
-
-    bias_here = x == y
-    for dq in (2, 1, 3):
-        q = (x + dq) % 4
-        send(
-            bias_pack.at[pl.ds(pl.multiple_of(16 * q, 16), 16)],
-            bias_recv.at[y],
-            misc_send.at[1],
-            misc_recv.at[1],
-            (z, 4 * q + x, core),
-        )
-    own_rows = pl.ds(pl.multiple_of(16 * x, 16), 16)
-    send_or_keep(
-        bias_here,
-        bias_pack.at[own_rows],
-        bias_recv.at[y],
-        misc_self.at[1],
-        misc_recv.at[1],
-        (z, 4 * x + x, core),
-    )
-
-    @pl.when(core == 0)
-    def _():
-        wait_for(leaf_relay, relay_sem.at[0])
-        send(leaf_relay, leaf_recv, relay_sem.at[1], misc_recv.at[0], (z, col, 1))
+        send_biases()
 
     wait_for(leaf_recv, misc_recv.at[0])
     wait_for(lower_inverse, weight_sem.at[0])
@@ -401,6 +402,15 @@
         recv1,
         0,
     )
+
+    @pl.when(core == 0)
+    def _():
+        pl.semaphore_wait(ready, 15 + 3)
+        pl.semaphore_signal(go, inc=1, device_id=(z, col, 1), device_id_type=MESH)
+        for u in range(4):
+            wait_for(leaf_relay.at[u], relay_sem.at[u])
+            send(leaf_relay.at[u], leaf_recv.at[u], relay_sem.at[4], misc_recv.at[0], (z, col, 1))
+
     wait_for(recv1, scatter_recv.at[0])
     leaf_value[...] = add_up(recv1, 16)
     part1[...] = leaf_value[...].astype(BF16)
@@ -623,7 +633,7 @@
 
     @pl.when(core == 0)
     def _():
-        wait_for(leaf_recv, relay_sem.at[1])
+        wait_for(leaf_recv, relay_sem.at[4])
         wait_sent_unless(leaf_here, leaf_recv.at[0], misc_self.at[0])
 
     @pl.when(core == 1)
@@ -704,7 +714,8 @@
         pltpu.SemaphoreType.DMA((4,)),
         pltpu.SemaphoreType.DMA((4,)),
         pltpu.SemaphoreType.DMA((5,)),
-        pltpu.SemaphoreType.DMA((2,)),
+        pltpu.SemaphoreType.DMA((5,)),
+        pltpu.SemaphoreType.REGULAR,
         pltpu.SemaphoreType.REGULAR,
         pltpu.SemaphoreType.REGULAR,
     ]

time: 109 us -> 110 us (level)
  no operation moved by 1% of the time
where the time goes in v4:
time: 110 us; the launch traced here: 109 us
  Pallas kernels  109 us (99%)
    pallas_call x1, Pallas kernels, per_device(): pl.pallas_call(kernel, name='tree_solve', out_shape=(pltpu.VMEM((3, 64, 6...  108 us

profile of v4, /device:TPU:0, one launch (start us, length us, event | category | flops | bytes accessed | tf_op | source)
XLA Modules:
  0.0 109.4 jit_solution(12253274080299446752)
XLA Ops:
  0.6 108.1 %tree_solve.1 = (f32[3,64,64]{2,1,0:T(8,128)S(1)}, f32[64,64]{1,0:T(8,128)S(1)}) custom-call(f32[3,64,64]{2,1,0:T(8,128)} %bitcast.12, f32[64,64]{1,0:T(8,128)} %rhs_root_hbm.1, s32[5,2,8]{2,1,0:T(2,128)} %bitcast.13, s32[5,2,8]{2,1,0:T(2,128)} %bitcast.14, bf16[5,256,1024]{2,1,0:T(8,128)(2,1)} %bitcast.8, bf16[5,256,1024]{2,1,0:T(8,128)(2,1)} %bitcast.9, ...), custom_call_target="tpu_custom_call" | custom-call | tf_op jit(solution)/shard_map/tree_solve/pallas_call | solution.py:722
  108.8 0.7 leave.1

commit v5 on v3

--- a/solution.py
+++ b/solution.py
@@ -554,15 +554,15 @@
     wait_for(vec8, spread_recv.at[7])
     vector = vec8[...].reshape(64, 256)
     vector9 = vector
-    multiply(
-        lambda j: [
-            second_early[s, :, columns_of(j)] + dot(vector9, block(upper.at[s], j))
-            for s in range(2)
-        ],
-        send9,
-        recv9,
-        8,
-    )
+    for s in range(2):
+        multiply(
+            lambda j, s=s: [
+                second_early[s, :, columns_of(j)] + dot(vector9, block(upper.at[s], j))
+            ],
+            send9.at[s],
+            recv9.at[s],
+            8 + 2 * s,
+        )
 
     odd = y % 2 == 1
     wait_for(root_out_recv, misc_recv.at[2])
@@ -572,46 +572,54 @@
     value = first_out_recv[...].reshape(64, 128)
     sol_half[0] = jnp.where(odd, value[:, 64:128], value[:, 0:64])
 
-    wait_for(recv9, scatter_recv.at[8])
-    part9[...] = (leaf_value[...] - add_up(recv9, 16)).astype(BF16)
-    spread(part9, vec9, 8)
-
-    wait_for(vec9, spread_recv.at[8])
-    second1 = vec9[:, 0].reshape(64, 256)
-    second2 = vec9[:, 1].reshape(64, 256)
-    for dx in (2, 1, 3, 0):
-        j = (x + dx) % 4
-        value1 = dot(second1, block(upper_inverse.at[1], j))
-        value2 = dot(second2, block(upper_inverse.at[2], j))
-        for u in range(4):
-            span = slice(64 * u, 64 * u + 64)
-            send10[4 * j + u] = jnp.concatenate([value1[:, span], value2[:, span]], axis=1).astype(
-                BF16
-            )
-        for dy in (2, 1, 3, 0):
-            peer = 4 * j + (y + dy) % 4
-            if dx or dy:
-                send(
-                    send10.at[peer],
-                    recv10.at[col],
-                    scatter_send.at[9],
-                    scatter_recv.at[9],
-                    (z, peer, core),
-                )
-            else:
-                start_local(send10.at[peer], recv10.at[col], scatter_recv.at[9])
-    wait_for(recv10, scatter_recv.at[9])
-    total = add_up(recv10, 16)
-    sol_half[1] = total[:, 0:64]
-    sol_half[2] = total[:, 64:128]
-
-    sends = (send1, send2, send3, None, send5, send6, send7, send8, send9, send10)
+    for s in range(2):
+        wait_for(recv9.at[s], scatter_recv.at[8 + 2 * s])
+        part9[s] = (leaf_value[s] - add_up(recv9.at[s], 16)).astype(BF16)
+        spread(part9.at[s], vec9.at[s], 8 + s)
+
+    for s in range(2):
+        wait_for(vec9.at[s], spread_recv.at[8 + s])
+        vector = vec9[s].reshape(64, 256)
+        for dx in (2, 1, 3, 0):
+            j = (x + dx) % 4
+            value = dot(vector, block(upper_inverse.at[1 + s], j))
+            for u in range(4):
+                span = slice(64 * u, 64 * u + 64)
+                send10[s, 4 * j + u] = jnp.concatenate(
+                    [value[0:32, span], value[32:64, span]], axis=1
+                ).astype(BF16)
+            for dy in (2, 1, 3, 0):
+                peer = 4 * j + (y + dy) % 4
+                if dx or dy:
+                    send(
+                        send10.at[s, peer],
+                        recv10.at[s, col],
+                        scatter_send.at[9 + 2 * s],
+                        scatter_recv.at[9 + 2 * s],
+                        (z, peer, core),
+                    )
+                else:
+                    start_local(
+                        send10.at[s, peer], recv10.at[s, col], scatter_recv.at[9 + 2 * s]
+                    )
+    for s in range(2):
+        wait_for(recv10.at[s], scatter_recv.at[9 + 2 * s])
+        total = add_up(recv10.at[s], 16)
+        sol_half[1 + s, 0:32] = total[:, 0:64]
+        sol_half[1 + s, 32:64] = total[:, 64:128]
+
+    sends = (send1, send2, send3, None, send5, send6, send7, send8)
     for stage, ref in enumerate(sends):
         if ref is not None:
             wait_for(ref.at[pl.ds(0, 15)], scatter_send.at[stage])
     wait_for(recv4.at[0], scatter_send.at[3])
     wait_for(recv4.at[1, pl.ds(0, 15)], scatter_send.at[3])
-    for stage, ref in enumerate((vec1, vec2, vec3, None, None, None, vec7, vec8, vec9)):
+    for s in range(2):
+        wait_for(send9.at[s, pl.ds(0, 15)], scatter_send.at[8 + 2 * s])
+        wait_for(send10.at[s, pl.ds(0, 15)], scatter_send.at[9 + 2 * s])
+        wait_for(vec9.at[s, pl.ds(0, 3)], spread_send.at[8 + s])
+        wait_sent_unless(x == z, vec9.at[s, 0], spread_self.at[8 + s])
+    for stage, ref in enumerate((vec1, vec2, vec3, None, None, None, vec7, vec8)):
         if ref is not None:
             wait_for(ref.at[pl.ds(0, 3)], spread_send.at[stage])
             wait_sent_unless(x == z, ref.at[0], spread_self.at[stage])
@@ -656,17 +664,25 @@
     one = (16, 256)
     two = (2, 16, 256)
     half = (16, 128)
-    stage_chunks = [two, one, one, None, half, half, one, one, two, (64, 128)]
-    exchange = [
-        pltpu.VMEM((2, 16) + half if chunk is None else (16,) + chunk, BF16)
-        for chunk in stage_chunks
+    stage_chunks = [
+        (16,) + two,
+        (16,) + one,
+        (16,) + one,
+        (2, 16) + half,
+        (16,) + half,
+        (16,) + half,
+        (16,) + one,
+        (16,) + one,
+        (2, 16) + one,
+        (2, 16, 32, 128),
     ]
+    exchange = [pltpu.VMEM(chunk, BF16) for chunk in stage_chunks]
     part_chunks = [two, one, one, half, half, half, one, one, two]
     parts = [pltpu.VMEM(chunk, BF16) for chunk in part_chunks]
     vectors = [
         pltpu.VMEM((2, 4) + chunk if chunk == half else (4,) + chunk, BF16)
-        for chunk in part_chunks
-    ]
+        for chunk in part_chunks[:8]
+    ] + [pltpu.VMEM((2, 4) + one, BF16)]
     scratch = [
         pltpu.VMEM((3, 64, 64), F32),
         pltpu.VMEM((64, 64), F32),
@@ -696,11 +712,11 @@
         pltpu.VMEM((2,) + half, F32),
         pltpu.VMEM((4,) + half, F32),
         pltpu.SemaphoreType.DMA((10,)),
+        pltpu.SemaphoreType.DMA((12,)),
+        pltpu.SemaphoreType.DMA((12,)),
         pltpu.SemaphoreType.DMA((10,)),
         pltpu.SemaphoreType.DMA((10,)),
-        pltpu.SemaphoreType.DMA((9,)),
-        pltpu.SemaphoreType.DMA((9,)),
-        pltpu.SemaphoreType.DMA((9,)),
+        pltpu.SemaphoreType.DMA((10,)),
         pltpu.SemaphoreType.DMA((4,)),
         pltpu.SemaphoreType.DMA((4,)),
         pltpu.SemaphoreType.DMA((5,)),

time: 109 us -> 109 us (level)
  no operation moved by 1% of the time
where the time goes in v5:
time: 109 us
  Pallas kernels  108 us (99%)
    pallas_call x1, Pallas kernels, per_device(): pl.pallas_call(kernel, name='tree_solve', out_shape=(pltpu.VMEM((3, 64, 6...  108 us

profile of v5, /device:TPU:0, one launch (start us, length us, event | category | flops | bytes accessed | tf_op | source)
XLA Modules:
  0.0 108.8 jit_solution(720613120432550178)
XLA Ops:
  0.6 107.5 %tree_solve.1 = (f32[3,64,64]{2,1,0:T(8,128)S(1)}, f32[64,64]{1,0:T(8,128)S(1)}) custom-call(f32[3,64,64]{2,1,0:T(8,128)} %bitcast.12, f32[64,64]{1,0:T(8,128)} %rhs_root_hbm.1, s32[5,2,8]{2,1,0:T(2,128)} %bitcast.13, s32[5,2,8]{2,1,0:T(2,128)} %bitcast.14, bf16[5,256,1024]{2,1,0:T(8,128)(2,1)} %bitcast.8, bf16[5,256,1024]{2,1,0:T(8,128)(2,1)} %bitcast.9, ...), custom_call_target="tpu_custom_call" | custom-call | tf_op jit(solution)/shard_map/tree_solve/pallas_call | solution.py:727
  108.2 0.7 leave.1

commit v6 on v5

--- a/solution.py
+++ b/solution.py
@@ -94,6 +94,7 @@
     vec9,
     leaf_value,
     top_value,
+    top_early,
     root_early,
     second_early,
     root_out,
@@ -395,22 +396,27 @@
         jnp.concatenate([p[:, 64 * s : 64 * s + 64] for p in pieces], axis=1).astype(BF16)
         for s in range(2)
     ]
+    for s in range(2):
+        multiply(
+            lambda j, s=s: [dot(leaves[s], block(lower_inverse.at[1 + s], j))],
+            send1.at[s],
+            recv1.at[s],
+            12 * s,
+        )
+    for s in range(2):
+        wait_for(recv1.at[s], scatter_recv.at[12 * s])
+        leaf_value[s] = add_up(recv1.at[s], 16)
+        part1[s] = leaf_value[s].astype(BF16)
+        spread(part1.at[s], vec1.at[s], 10 * s)
+
+    wait_for(vec1.at[0], spread_recv.at[0])
+    leaf1 = vec1[0].reshape(64, 256)
+    for j in range(4):
+        top_early[:, 256 * j : 256 * j + 256] = dot(leaf1, block(lower.at[0], j))
+    wait_for(vec1.at[1], spread_recv.at[10])
+    leaf2 = vec1[1].reshape(64, 256)
     multiply(
-        lambda j: [dot(leaves[s], block(lower_inverse.at[1 + s], j)) for s in range(2)],
-        send1,
-        recv1,
-        0,
-    )
-    wait_for(recv1, scatter_recv.at[0])
-    leaf_value[...] = add_up(recv1, 16)
-    part1[...] = leaf_value[...].astype(BF16)
-    spread(part1, vec1, 0)
-
-    wait_for(vec1, spread_recv.at[0])
-    leaf1 = vec1[:, 0].reshape(64, 256)
-    leaf2 = vec1[:, 1].reshape(64, 256)
-    multiply(
-        lambda j: [dot(leaf1, block(lower.at[0], j)) + dot(leaf2, block(lower.at[1], j))],
+        lambda j: [top_early[:, columns_of(j)] + dot(leaf2, block(lower.at[1], j))],
         send2,
         recv2,
         1,
@@ -608,18 +614,21 @@
         sol_half[1 + s, 0:32] = total[:, 0:64]
         sol_half[1 + s, 32:64] = total[:, 64:128]
 
-    sends = (send1, send2, send3, None, send5, send6, send7, send8)
+    sends = (None, send2, send3, None, send5, send6, send7, send8)
     for stage, ref in enumerate(sends):
         if ref is not None:
             wait_for(ref.at[pl.ds(0, 15)], scatter_send.at[stage])
     wait_for(recv4.at[0], scatter_send.at[3])
     wait_for(recv4.at[1, pl.ds(0, 15)], scatter_send.at[3])
     for s in range(2):
+        wait_for(send1.at[s, pl.ds(0, 15)], scatter_send.at[12 * s])
+        wait_for(vec1.at[s, pl.ds(0, 3)], spread_send.at[10 * s])
+        wait_sent_unless(x == z, vec1.at[s, 0], spread_self.at[10 * s])
         wait_for(send9.at[s, pl.ds(0, 15)], scatter_send.at[8 + 2 * s])
         wait_for(send10.at[s, pl.ds(0, 15)], scatter_send.at[9 + 2 * s])
         wait_for(vec9.at[s, pl.ds(0, 3)], spread_send.at[8 + s])
         wait_sent_unless(x == z, vec9.at[s, 0], spread_self.at[8 + s])
-    for stage, ref in enumerate((vec1, vec2, vec3, None, None, None, vec7, vec8)):
+    for stage, ref in enumerate((None, vec2, vec3, None, None, None, vec7, vec8)):
         if ref is not None:
             wait_for(ref.at[pl.ds(0, 3)], spread_send.at[stage])
             wait_sent_unless(x == z, ref.at[0], spread_self.at[stage])
@@ -665,7 +674,7 @@
     two = (2, 16, 256)
     half = (16, 128)
     stage_chunks = [
-        (16,) + two,
+        (2, 16) + one,
         (16,) + one,
         (16,) + one,
         (2, 16) + half,
@@ -681,8 +690,9 @@
     parts = [pltpu.VMEM(chunk, BF16) for chunk in part_chunks]
     vectors = [
         pltpu.VMEM((2, 4) + chunk if chunk == half else (4,) + chunk, BF16)
-        for chunk in part_chunks[:8]
-    ] + [pltpu.VMEM((2, 4) + one, BF16)]
+        for chunk in part_chunks[1:8]
+    ]
+    vectors = [pltpu.VMEM((2, 4) + one, BF16), *vectors, pltpu.VMEM((2, 4) + one, BF16)]
     scratch = [
         pltpu.VMEM((3, 64, 64), F32),
         pltpu.VMEM((64, 64), F32),
@@ -706,17 +716,18 @@
         pltpu.VMEM(two, F32),
         pltpu.VMEM(one, F32),
         pltpu.VMEM((64, 1024), F32),
+        pltpu.VMEM((64, 1024), F32),
         pltpu.VMEM((2, 64, 1024), F32),
         pltpu.VMEM(half, F32),
         pltpu.VMEM((4,) + half, F32),
         pltpu.VMEM((2,) + half, F32),
         pltpu.VMEM((4,) + half, F32),
         pltpu.SemaphoreType.DMA((10,)),
-        pltpu.SemaphoreType.DMA((12,)),
-        pltpu.SemaphoreType.DMA((12,)),
-        pltpu.SemaphoreType.DMA((10,)),
-        pltpu.SemaphoreType.DMA((10,)),
-        pltpu.SemaphoreType.DMA((10,)),
+        pltpu.SemaphoreType.DMA((13,)),
+        pltpu.SemaphoreType.DMA((13,)),
+        pltpu.SemaphoreType.DMA((11,)),
+        pltpu.SemaphoreType.DMA((11,)),
+        pltpu.SemaphoreType.DMA((11,)),
         pltpu.SemaphoreType.DMA((4,)),
         pltpu.SemaphoreType.DMA((4,)),
         pltpu.SemaphoreType.DMA((5,)),

time: 109 us -> 108 us (level)
  no operation moved by 1% of the time
where the time goes in v6:
time: 108 us
  Pallas kernels  107 us (99%)
    pallas_call x1, Pallas kernels, per_device(): pl.pallas_call(kernel, name='tree_solve', out_shape=(pltpu.VMEM((3, 64, 6...  107 us

profile of v6, /device:TPU:0, one launch (start us, length us, event | category | flops | bytes accessed | tf_op | source)
XLA Modules:
  0.0 108.0 jit_solution(542415024164808867)
XLA Ops:
  0.6 106.6 %tree_solve.1 = (f32[3,64,64]{2,1,0:T(8,128)S(1)}, f32[64,64]{1,0:T(8,128)S(1)}) custom-call(f32[3,64,64]{2,1,0:T(8,128)} %bitcast.12, f32[64,64]{1,0:T(8,128)} %rhs_root_hbm.1, s32[5,2,8]{2,1,0:T(2,128)} %bitcast.13, s32[5,2,8]{2,1,0:T(2,128)} %bitcast.14, bf16[5,256,1024]{2,1,0:T(8,128)(2,1)} %bitcast.8, bf16[5,256,1024]{2,1,0:T(8,128)(2,1)} %bitcast.9, ...), custom_call_target="tpu_custom_call" | custom-call | tf_op jit(solution)/shard_map/tree_solve/pallas_call | solution.py:738
  107.3 0.7 leave.1

commit v7 on v6

--- a/solution.py
+++ b/solution.py
@@ -252,7 +252,7 @@
                 leaf_pack,
                 leaf_relay.at[y],
                 misc_send.at[0],
-                relay_sem.at[0],
+                relay_sem.at[y],
                 ((z + dz) % 4, 4 * z + x, 0),
             )
 
@@ -386,8 +386,9 @@
 
     @pl.when(core == 0)
     def _():
-        wait_for(leaf_relay, relay_sem.at[0])
-        send(leaf_relay, leaf_recv, relay_sem.at[1], misc_recv.at[0], (z, col, 1))
+        for u in range(4):
+            wait_for(leaf_relay.at[u], relay_sem.at[u])
+            send(leaf_relay.at[u], leaf_recv.at[u], relay_sem.at[4], misc_recv.at[0], (z, col, 1))
 
     wait_for(leaf_recv, misc_recv.at[0])
     wait_for(lower_inverse, weight_sem.at[0])
@@ -608,12 +609,6 @@
                     start_local(
                         send10.at[s, peer], recv10.at[s, col], scatter_recv.at[9 + 2 * s]
                     )
-    for s in range(2):
-        wait_for(recv10.at[s], scatter_recv.at[9 + 2 * s])
-        total = add_up(recv10.at[s], 16)
-        sol_half[1 + s, 0:32] = total[:, 0:64]
-        sol_half[1 + s, 32:64] = total[:, 64:128]
-
     sends = (None, send2, send3, None, send5, send6, send7, send8)
     for stage, ref in enumerate(sends):
         if ref is not None:
@@ -625,7 +620,6 @@
         wait_for(vec1.at[s, pl.ds(0, 3)], spread_send.at[10 * s])
         wait_sent_unless(x == z, vec1.at[s, 0], spread_self.at[10 * s])
         wait_for(send9.at[s, pl.ds(0, 15)], scatter_send.at[8 + 2 * s])
-        wait_for(send10.at[s, pl.ds(0, 15)], scatter_send.at[9 + 2 * s])
         wait_for(vec9.at[s, pl.ds(0, 3)], spread_send.at[8 + s])
         wait_sent_unless(x == z, vec9.at[s, 0], spread_self.at[8 + s])
     for stage, ref in enumerate((None, vec2, vec3, None, None, None, vec7, vec8)):
@@ -640,7 +634,7 @@
 
     @pl.when(core == 0)
     def _():
-        wait_for(leaf_recv, relay_sem.at[1])
+        wait_for(leaf_recv, relay_sem.at[4])
         wait_sent_unless(leaf_here, leaf_recv.at[0], misc_self.at[0])
 
     @pl.when(core == 1)
@@ -654,6 +648,14 @@
         wait_sent_unless(out_here(k, core), root_out_recv.at[0], misc_self.at[2 + k])
     wait_for(first_out_recv.at[pl.ds(0, 3)], misc_send.at[3])
     wait_sent_unless(first_here, first_out_recv.at[0], misc_self.at[4])
+
+    for s in range(2):
+        wait_for(recv10.at[s], scatter_recv.at[9 + 2 * s])
+        total = add_up(recv10.at[s], 16)
+        sol_half[1 + s, 0:32] = total[:, 0:64]
+        sol_half[1 + s, 32:64] = total[:, 64:128]
+    for s in range(2):
+        wait_for(send10.at[s, pl.ds(0, 15)], scatter_send.at[9 + 2 * s])
 
 
 def per_device(
@@ -731,7 +733,7 @@
         pltpu.SemaphoreType.DMA((4,)),
         pltpu.SemaphoreType.DMA((4,)),
         pltpu.SemaphoreType.DMA((5,)),
-        pltpu.SemaphoreType.DMA((2,)),
+        pltpu.SemaphoreType.DMA((5,)),
         pltpu.SemaphoreType.REGULAR,
         pltpu.SemaphoreType.REGULAR,
     ]

time: 108 us -> 108 us (level)
  no operation moved by 1% of the time
where the time goes in v7:
time: 108 us
  Pallas kernels  107 us (99%)
    pallas_call x1, Pallas kernels, per_device(): pl.pallas_call(kernel, name='tree_solve', out_shape=(pltpu.VMEM((3, 64, 6...  107 us

profile of v7, /device:TPU:0, one launch (start us, length us, event | category | flops | bytes accessed | tf_op | source)
XLA Modules:
  0.0 107.9 jit_solution(16043652237857317269)
XLA Ops:
  0.6 106.6 %tree_solve.1 = (f32[3,64,64]{2,1,0:T(8,128)S(1)}, f32[64,64]{1,0:T(8,128)S(1)}) custom-call(f32[3,64,64]{2,1,0:T(8,128)} %bitcast.12, f32[64,64]{1,0:T(8,128)} %rhs_root_hbm.1, s32[5,2,8]{2,1,0:T(2,128)} %bitcast.13, s32[5,2,8]{2,1,0:T(2,128)} %bitcast.14, bf16[5,256,1024]{2,1,0:T(8,128)(2,1)} %bitcast.8, bf16[5,256,1024]{2,1,0:T(8,128)(2,1)} %bitcast.9, ...), custom_call_target="tpu_custom_call" | custom-call | tf_op jit(solution)/shard_map/tree_solve/pallas_call | solution.py:740
  107.2 0.7 leave.1

commit v8 on v7

--- a/solution.py
+++ b/solution.py
@@ -182,21 +182,6 @@
     start_local(rhs_root_hbm, rhs_root, weight_sem.at[7])
     start_local(lower_pattern_hbm, lower_pattern, weight_sem.at[8])
     start_local(upper_pattern_hbm, upper_pattern, weight_sem.at[9])
-    start_local(lower_inverse_hbm, lower_inverse, weight_sem.at[0])
-    start_local(lower_hbm, lower, weight_sem.at[1])
-    for j in range(4):
-        columns = pl.ds(pl.multiple_of(256 * j + 128 * core, 128), 128)
-        start_local(
-            root_lower_hbm.at[:, columns], root_lower.at[:, pl.ds(128 * j, 128)], weight_sem.at[2]
-        )
-    for j in range(4):
-        columns = pl.ds(pl.multiple_of(256 * j + 128 * core, 128), 128)
-        start_local(
-            root_upper_hbm.at[:, columns], root_upper.at[:, pl.ds(128 * j, 128)], weight_sem.at[3]
-        )
-    start_local(upper_hbm, upper, weight_sem.at[4])
-    start_local(upper_inverse_hbm, upper_inverse, weight_sem.at[5])
-
     wait_for(rhs_half, weight_sem.at[6])
     wait_for(rhs_root, weight_sem.at[7])
     leaf_pack[...] = jnp.concatenate([rhs_half[1], rhs_half[2]], axis=1).astype(BF16)
@@ -255,6 +240,21 @@
                 relay_sem.at[y],
                 ((z + dz) % 4, 4 * z + x, 0),
             )
+
+    start_local(lower_inverse_hbm, lower_inverse, weight_sem.at[0])
+    start_local(lower_hbm, lower, weight_sem.at[1])
+    for j in range(4):
+        columns = pl.ds(pl.multiple_of(256 * j + 128 * core, 128), 128)
+        start_local(
+            root_lower_hbm.at[:, columns], root_lower.at[:, pl.ds(128 * j, 128)], weight_sem.at[2]
+        )
+    for j in range(4):
+        columns = pl.ds(pl.multiple_of(256 * j + 128 * core, 128), 128)
+        start_local(
+            root_upper_hbm.at[:, columns], root_upper.at[:, pl.ds(128 * j, 128)], weight_sem.at[3]
+        )
+    start_local(upper_hbm, upper, weight_sem.at[4])
+    start_local(upper_inverse_hbm, upper_inverse, weight_sem.at[5])
 
     def scatter(src, dst, stage):
         for dx, dy in NEAR:

time: 108 us -> 108 us (level)
  no operation moved by 1% of the time
where the time goes in v8:
time: 108 us
  Pallas kernels  107 us (99%)
    pallas_call x1, Pallas kernels, per_device(): pl.pallas_call(kernel, name='tree_solve', out_shape=(pltpu.VMEM((3, 64, 6...  107 us

profile of v8, /device:TPU:0, one launch (start us, length us, event | category | flops | bytes accessed | tf_op | source)
XLA Modules:
  0.0 107.9 jit_solution(1742120963644279076)
XLA Ops:
  0.6 106.6 %tree_solve.1 = (f32[3,64,64]{2,1,0:T(8,128)S(1)}, f32[64,64]{1,0:T(8,128)S(1)}) custom-call(f32[3,64,64]{2,1,0:T(8,128)} %bitcast.12, f32[64,64]{1,0:T(8,128)} %rhs_root_hbm.1, s32[5,2,8]{2,1,0:T(2,128)} %bitcast.13, s32[5,2,8]{2,1,0:T(2,128)} %bitcast.14, bf16[5,256,1024]{2,1,0:T(8,128)(2,1)} %bitcast.8, bf16[5,256,1024]{2,1,0:T(8,128)(2,1)} %bitcast.9, ...), custom_call_target="tpu_custom_call" | custom-call | tf_op jit(solution)/shard_map/tree_solve/pallas_call | solution.py:740
  107.2 0.7 leave.1

commit v9 on v7

--- a/solution.py
+++ b/solution.py
@@ -20,10 +20,10 @@
 
 
 def add_up(ref, count):
-    total = ref[0].astype(F32)
-    for i in range(1, count):
-        total = total + ref[i].astype(F32)
-    return total
+    terms = [ref[i].astype(F32) for i in range(count)]
+    while len(terms) > 1:
+        terms = [terms[i] + terms[i + 1] for i in range(0, len(terms), 2)]
+    return terms[0]
 
 
 def kernel(

time: 108 us -> 108 us (level)
  no operation moved by 1% of the time
where the time goes in v9:
time: 108 us
  Pallas kernels  107 us (99%)
    pallas_call x1, Pallas kernels, per_device(): pl.pallas_call(kernel, name='tree_solve', out_shape=(pltpu.VMEM((3, 64, 6...  107 us

profile of v9, /device:TPU:0, one launch (start us, length us, event | category | flops | bytes accessed | tf_op | source)
XLA Modules:
  0.0 107.9 jit_solution(13858060819640943989)
XLA Ops:
  0.6 106.6 %tree_solve.1 = (f32[3,64,64]{2,1,0:T(8,128)S(1)}, f32[64,64]{1,0:T(8,128)S(1)}) custom-call(f32[3,64,64]{2,1,0:T(8,128)} %bitcast.12, f32[64,64]{1,0:T(8,128)} %rhs_root_hbm.1, s32[5,2,8]{2,1,0:T(2,128)} %bitcast.13, s32[5,2,8]{2,1,0:T(2,128)} %bitcast.14, bf16[5,256,1024]{2,1,0:T(8,128)(2,1)} %bitcast.8, bf16[5,256,1024]{2,1,0:T(8,128)(2,1)} %bitcast.9, ...), custom_call_target="tpu_custom_call" | custom-call | tf_op jit(solution)/shard_map/tree_solve/pallas_call | solution.py:740
  107.2 0.7 leave.1
